TPU v7x, 512 devices: a whole 4x8x8 slice. The times are simulated.
512 devices in a mesh: blk: 16 (over z_lo, x), leaf: 32 (over y, z_hi, core).
Axes of the slice: x: 4, y: 8, z: 8 (z_hi: 2, z_lo: 4; z = z_hi * 4 + z_lo), core: 2. Of those that a mesh axis runs over, the one named last changes fastest.
Arguments:
- points: bfloat16 [3, 262144], P(None, ('blk', 'leaf')), may hold values from 0 to 1
- test_matrix: bfloat16 [262144, 512], P(('blk', 'leaf')), may hold values from -6 to 6
- near_lists: int32 [1024, 5], P(('blk', 'leaf')), may hold values from 0 to 5, as said below
- leaf_pivots: int32 [512, 256], P(('blk', 'leaf')), may hold values from 0 to 511, as said below
- leaf_proj: bfloat16 [262144, 256], P(('blk', 'leaf')), may hold values from -0.25 to 0.25
- merge_pivots: int32 [3, 512, 256], P(None, ('blk', 'leaf')), may hold values from 0 to 511, as said below
- merge_proj: bfloat16 [3, 512, 512, 256], P(None, ('blk', 'leaf')), as said below
Outputs:
- sample: bfloat16 [262144, 512], P(('blk', 'leaf'))
- top_samples: float32 [131072, 512], P(('blk', 'leaf'))
- top_omega: float32 [131072, 512], P(('blk', 'leaf'))
Inputs may be any that keep to these rules, and one draw needn't show every extreme that they name: `near_lists`: the 5 entries of one row are distinct. `leaf_pivots`: the 256 entries of one row are distinct. `merge_pivots`: the 256 entries of one row are distinct; rows [t, n] are equal for all n with the same n // 2^(t+1). `merge_proj`: matrices [t, n] are equal for all n with the same n // 2^(t+1); entries lie within -4 / sqrt(512) to 4 / sqrt(512).
All inputs are finite; a program needn't handle non-finite values.
Results may differ from a plain program's by a relative error of at most 0.0048.
Values may be sent and summed in bfloat16 or wider, within the bound.
A program may use at most 64 MiB of HBM per device.

v0:
```python
import math

import jax
import jax.numpy as jnp
from jax import lax
from jax.sharding import PartitionSpec as P

SPREAD = 25.0


def shifted(block, axis, distance):
    devices = range(lax.axis_size(axis))
    route = [((i - distance) % len(devices), i) for i in devices]
    return lax.ppermute(block, axis, route)


def swapped(block, axis, stride):
    count = lax.axis_size(axis)
    route = []
    for low in range(count):
        high = low | 1 << stride
        if high != low and high < count:
            route += [(low, high), (high, low)]
    return lax.ppermute(block, axis, route)


def kernel_block(row_points, col_points):
    offsets = row_points[..., :, :, None] - col_points[..., :, None, :]
    return jnp.exp(-SPREAD * jnp.sum(offsets * offsets, axis=-3))


def to_blocks(raw_points, block_count, block_rows):
    return jnp.transpose(
        raw_points.astype(jnp.float32).reshape(3, block_count, block_rows), (1, 0, 2)
    )


def on_device(points, test_matrix, near_lists, leaf_pivots, leaf_proj, merge_pivots, merge_proj):
    row_count = test_matrix.shape[0]
    sample_count = test_matrix.shape[1]
    block_count = near_lists.shape[0]
    slot_count = near_lists.shape[1]
    block_rows = row_count // block_count
    skel_rank = leaf_pivots.shape[1]
    level_count = merge_pivots.shape[0]
    near_amp = 9.0 / math.sqrt(slot_count * block_rows)
    far_amp = 3.0 / math.sqrt(skel_rank)
    highest = lax.Precision.HIGHEST
    own_points = to_blocks(points, block_count, block_rows)
    behind_matrix, behind_points = shifted((test_matrix, points), "blk", 1)
    ahead_matrix, ahead_points = shifted((test_matrix, points), "blk", -1)
    wide_blocks = jnp.concatenate([behind_matrix, test_matrix, ahead_matrix], axis=0).reshape(
        3 * block_count, block_rows, sample_count
    )
    wide_points = jnp.concatenate(
        [
            to_blocks(behind_points, block_count, block_rows),
            own_points,
            to_blocks(ahead_points, block_count, block_rows),
        ],
        axis=0,
    )
    full_sum = jnp.zeros((block_count, block_rows, sample_count), jnp.float32)
    remote_sum = jnp.zeros((block_count, block_rows, sample_count), jnp.float32)
    for entry_slot in range(slot_count):
        candidate = near_lists[:, entry_slot]
        near_block = (
            near_amp * kernel_block(own_points, jnp.take(wide_points, candidate, axis=0))
        ).astype(jnp.bfloat16)
        term_block = jnp.einsum(
            "ipq,iqr->ipr",
            near_block,
            jnp.take(wide_blocks, candidate, axis=0),
            preferred_element_type=jnp.float32,
        )
        is_remote = (candidate // block_count != 1).astype(jnp.float32)[:, None, None]
        full_sum = full_sum + term_block
        remote_sum = remote_sum + is_remote * term_block
    full_sum = full_sum.reshape(row_count, sample_count)
    remote_sum = remote_sum.reshape(row_count, sample_count)
    sample = full_sum.astype(jnp.bfloat16)
    pivots = leaf_pivots[0]
    samples = jnp.take(remote_sum, pivots, axis=0)
    skeleton = jnp.take(points.astype(jnp.float32), pivots, axis=1)
    compressed = lax.dot_general(
        leaf_proj, test_matrix, (((0,), (0,)), ((), ())), preferred_element_type=jnp.float32
    )
    position = lax.axis_index("leaf")
    for tree_level in range(level_count):
        other_samples, other_compressed, other_skeleton = swapped(
            (samples, compressed, skeleton), "leaf", tree_level
        )
        is_left = position >> tree_level & 1 == 0
        left_samples = jnp.where(is_left, samples, other_samples)
        right_samples = jnp.where(is_left, other_samples, samples)
        left_compressed = jnp.where(is_left, compressed, other_compressed)
        right_compressed = jnp.where(is_left, other_compressed, compressed)
        left_skeleton = jnp.where(is_left, skeleton, other_skeleton)
        right_skeleton = jnp.where(is_left, other_skeleton, skeleton)
        coupling = far_amp * kernel_block(left_skeleton, right_skeleton)
        upper_half = left_samples - jnp.dot(coupling, right_compressed, precision=highest)
        lower_half = right_samples - lax.dot_general(
            coupling, left_compressed, (((0,), (0,)), ((), ())), precision=highest
        )
        stacked = jnp.concatenate([upper_half, lower_half], axis=0)
        node_pivots = merge_pivots[tree_level, 0]
        samples = jnp.take(stacked, node_pivots, axis=0)
        skeleton = jnp.take(
            jnp.concatenate([left_skeleton, right_skeleton], axis=1), node_pivots, axis=1
        )
        projection = merge_proj[tree_level, 0].astype(jnp.float32)
        compressed = lax.dot_general(
            projection,
            jnp.concatenate([left_compressed, right_compressed], axis=0),
            (((0,), (0,)), ((), ())),
            precision=highest,
        )
    return (sample, samples, compressed)


def solution(mesh):
    placed = (
        P(None, ("blk", "leaf")),
        P(("blk", "leaf"), None),
        P(("blk", "leaf"), None),
        P(("blk", "leaf"), None),
        P(("blk", "leaf"), None),
        P(None, ("blk", "leaf"), None),
        P(None, ("blk", "leaf"), None, None),
    )
    return jax.shard_map(
        on_device,
        mesh=mesh,
        in_specs=placed,
        out_specs=(P(("blk", "leaf"), None), P(("blk", "leaf"), None), P(("blk", "leaf"), None)),
        check_vma=False,
    )
```

profile of v0, /device:TPU:1, one launch (start us, length us, event | category | flops | bytes accessed | tf_op | source)
XLA Modules:
  0.0 152.5 jit_solution(13926561694983911041)
XLA Ops:
  0.6 10.8 %collective-permute-start.3 = (bf16[512,512]{1,0:T(8,128)(2,1)}, bf16[512,512]{1,0:T(8,128)(2,1)S(1)}, u32[]{:S(2)}, u32[]{:S(2)}) collective-permute-start(bf16[512,512]{1,0:T(8,128)(2,1)} %param.16), channel_id=1, source_target_pairs={{32,0},{64,32},{96,64},{128,96},{160,128},{192,160},{224,192},{256... | collective-permute-start | bytes 1572872 | tf_op jit(solution)/shard_map/ppermute | solution.py:14
  11.4 1.9 %collective-permute-start.2 = (bf16[512,512]{1,0:T(8,128)(2,1)}, bf16[512,512]{1,0:T(8,128)(2,1)}, u32[]{:S(2)}, u32[]{:S(2)}) collective-permute-start(bf16[512,512]{1,0:T(8,128)(2,1)} %param.16), channel_id=1, source_target_pairs={{480,0},{0,32},{32,64},{64,96},{96,128},{128,160},{160,192},{192,2... | collective-permute-start | bytes 1572872 | tf_op jit(solution)/shard_map/ppermute | solution.py:14
  13.4 7.3 %collective-permute-start.1 = (bf16[3,512]{1,0:T(4,128)(2,1)}, bf16[3,512]{1,0:T(4,128)(2,1)S(1)}, u32[]{:S(2)}, u32[]{:S(2)}) collective-permute-start(bf16[3,512]{1,0:T(4,128)(2,1)} %param.15), channel_id=1, source_target_pairs={{32,0},{64,32},{96,64},{128,96},{160,128},{192,160},{224,192},{256... | collective-permute-start | bytes 9224 | tf_op jit(solution)/shard_map/ppermute | solution.py:14
  20.6 1.9 %collective-permute-start = (bf16[3,512]{1,0:T(4,128)(2,1)}, bf16[3,512]{1,0:T(4,128)(2,1)S(1)}, u32[]{:S(2)}, u32[]{:S(2)}) collective-permute-start(bf16[3,512]{1,0:T(4,128)(2,1)} %param.15), channel_id=1, source_target_pairs={{480,0},{0,32},{32,64},{64,96},{96,128},{128,160},{160,192},{192,2... | collective-permute-start | bytes 9224 | tf_op jit(solution)/shard_map/ppermute | solution.py:14
  25.7 3.4 %collective-permute-start.5 = (f32[3,256]{0,1:T(8,128)S(1)}, f32[3,256]{0,1:T(8,128)S(1)}, u32[]{:S(2)}, u32[]{:S(2)}) collective-permute-start(f32[3,256]{0,1:T(8,128)S(1)} %select_bitcast_fusion.2), channel_id=1, source_target_pairs={{0,1},{1,0},{2,3},{3,2},{4,5},{5,4},{6,7},{7,6},{8,9},{9,8},{10,11... | collective-permute-start | bytes 9224 | tf_op jit(solution)/shard_map/ppermute | solution.py:24
  31.7 1.4 fusion.94
  33.3 1.9 %collective-permute-start.6 = (f32[256,512]{1,0:T(8,128)S(1)}, f32[256,512]{1,0:T(8,128)}, u32[]{:S(2)}, u32[]{:S(2)}) collective-permute-start(f32[256,512]{1,0:T(8,128)S(1)} %fusion.94), channel_id=1, source_target_pairs={{0,1},{1,0},{2,3},{3,2},{4,5},{5,4},{6,7},{7,6},{8,9},{9,8},{10,11... | collective-permute-start | bytes 1572872 | tf_op jit(solution)/shard_map/ppermute | solution.py:24
  39.3 7.9 %collective-permute-start.8 = (f32[3,256]{0,1:T(8,128)S(1)}, f32[3,256]{0,1:T(8,128)S(1)}, u32[]{:S(2)}, u32[]{:S(2)}) collective-permute-start(f32[3,256]{0,1:T(8,128)S(1)} %select_bitcast_fusion.1), channel_id=1, source_target_pairs={{0,2},{2,0},{1,3},{3,1},{4,6},{6,4},{5,7},{7,5},{8,10},{10,8},{9,1... | collective-permute-start | bytes 9224 | tf_op jit(solution)/shard_map/ppermute | solution.py:24
  47.6 2.3 %multiply_reduce_fusion.3 = (f32[2,256,256]{2,1,0:T(8,128)}, f32[2,256,256]{2,1,0:T(8,128)}, f32[2,256,256]{2,1,0:T(8,128)}, f32[2,256,256]{2,1,0:T(8,128)}, f32[2,256,256]{2,1,0:T(8,128)}) fusion(f32[2,3,256]{2,1,0:T(4,128)S(1)} %broadcast_select_fusion.19, f32[2,3,256]{2,1,0:T(4,128)S(1)} %copy.70, f32[2,3,256]{2,1,0:T(4,128)S(1)} %broadcast_select_fusion.18, ...), kind=kLoop, calls=%fused_computation.21 | loop fusion | flops 5242880 | bytes 2658304 | tf_op jit(solution)/shard_map/reduce_sum | solution.py:29
  50.1 3.4 %collective-permute-done.8 = f32[3,256]{0,1:T(8,128)S(1)} collective-permute-done((f32[3,256]{0,1:T(8,128)S(1)}, f32[3,256]{0,1:T(8,128)S(1)}, u32[]{:S(2)}, u32[]{:S(2)}) %collective-permute-start.8) | collective-permute-done | bytes 3104 | tf_op jit(solution)/shard_map/ppermute | solution.py:24
  55.3 3.2 %collective-permute-start.11 = (f32[3,256]{0,1:T(8,128)}, f32[3,256]{0,1:T(8,128)}, u32[]{:S(2)}, u32[]{:S(2)}) collective-permute-start(f32[3,256]{0,1:T(8,128)} %select_bitcast_fusion), channel_id=1, source_target_pairs={{0,4},{4,0},{1,5},{5,1},{2,6},{6,2},{3,7},{7,3},{8,12},{12,8},{9,1... | collective-permute-start | bytes 9224 | tf_op jit(solution)/shard_map/ppermute | solution.py:24
  59.3 1.3 pad_maximum_fusion
  60.6 1.4 gather_fusion.7
  61.9 1.4 gather_fusion.5
  63.3 1.4 gather_fusion.3
  65.3 1.4 gather_fusion.9
  66.7 1.7 %fusion.11 = f32[2,256,512]{2,1,0:T(8,128)S(1)} fusion(bf16[2,256,512]{2,1,0:T(8,128)(2,1)} %gather_fusion.7, pred[2]{0:T(512)(128)(4,1)S(1)} %get-tuple-element.56, f32[2,256,256]{2,1,0:T(8,128)} %get-tuple-element.21), kind=kOutput, calls=%fused_computation.45 | convolution fusion | flops 134873088 | bytes 2097154 | tf_op jit(solution)/shard_map/ipq,iqr->ipr/dot_general | solution.py:70
  71.1 1.5 multiply_add_fusion
  73.7 3.2 %collective-permute-start.4 = (f32[256,512]{1,0:T(8,128)S(1)}, f32[256,512]{1,0:T(8,128)S(1)}, u32[]{:S(2)}, u32[]{:S(2)}) collective-permute-start(f32[256,512]{1,0:T(8,128)S(1)} %broadcast_select_fusion.3), channel_id=1, source_target_pairs={{0,1},{1,0},{2,3},{3,2},{4,5},{5,4},{6,7},{7,6},{8,9},{9,8},{10,11... | collective-permute-start | bytes 1572872 | tf_op jit(solution)/shard_map/ppermute | solution.py:24
  77.1 1.1 broadcast_select_fusion.5
  78.2 1.6 %convolution_bitcast_fusion.2 = f32[256,512]{1,0:T(8,128)S(1)} fusion(f32[256,512]{1,0:T(8,128)S(1)} %get-tuple-element.35, f32[256,512]{1,0:T(8,128)S(1)} %get-tuple-element.36, bf16[3,1,512,256]{3,2,1,0:T(8,128)(2,1)} %param.21), kind=kOutput, calls=%fused_computation.25 | convolution fusion | flops 805568512 | bytes 1835008 | tf_op jit(solution)/shard_map/dot_general | solution.py:112
  79.9 4.5 %collective-permute-start.9 = (f32[256,512]{1,0:T(8,128)S(1)}, f32[256,512]{1,0:T(8,128)}, u32[]{:S(2)}, u32[]{:S(2)}) collective-permute-start(f32[256,512]{1,0:T(8,128)S(1)} %convolution_bitcast_fusion.2), channel_id=1, source_target_pairs={{0,2},{2,0},{1,3},{3,1},{4,6},{6,4},{5,7},{7,5},{8,10},{10,8},{9,1... | collective-permute-start | bytes 1572872 | tf_op jit(solution)/shard_map/ppermute | solution.py:24
  86.9 4.7 %collective-permute-start.7 = (f32[256,512]{1,0:T(8,128)S(1)}, f32[256,512]{1,0:T(8,128)S(1)}, u32[]{:S(2)}, u32[]{:S(2)}) collective-permute-start(f32[256,512]{1,0:T(8,128)S(1)} %broadcast_select_fusion.2), channel_id=1, source_target_pairs={{0,2},{2,0},{1,3},{3,1},{4,6},{6,4},{5,7},{7,5},{8,10},{10,8},{9,1... | collective-permute-start | bytes 1572872 | tf_op jit(solution)/shard_map/ppermute | solution.py:24
  92.8 27.0 %collective-permute-done.9 = f32[256,512]{1,0:T(8,128)} collective-permute-done((f32[256,512]{1,0:T(8,128)S(1)}, f32[256,512]{1,0:T(8,128)}, u32[]{:S(2)}, u32[]{:S(2)}) %collective-permute-start.9) | collective-permute-done | bytes 524320 | tf_op jit(solution)/shard_map/ppermute | solution.py:24
  121.0 1.6 %convolution_bitcast_fusion.1 = f32[256,512]{1,0:T(8,128)S(1)} fusion(f32[256,512]{1,0:T(8,128)S(1)} %get-tuple-element.33, f32[256,512]{1,0:T(8,128)S(1)} %get-tuple-element.34, bf16[3,1,512,256]{3,2,1,0:T(8,128)(2,1)} %param.21), kind=kOutput, calls=%fused_computation.24 | convolution fusion | flops 805568512 | bytes 1835008 | tf_op jit(solution)/shard_map/dot_general | solution.py:112
  122.6 2.3 %collective-permute-start.12 = (f32[256,512]{1,0:T(8,128)S(1)}, f32[256,512]{1,0:T(8,128)}, u32[]{:S(2)}, u32[]{:S(2)}) collective-permute-start(f32[256,512]{1,0:T(8,128)S(1)} %convolution_bitcast_fusion.1), channel_id=1, source_target_pairs={{0,4},{4,0},{1,5},{5,1},{2,6},{6,2},{3,7},{7,3},{8,12},{12,8},{9,1... | collective-permute-start | bytes 1572872 | tf_op jit(solution)/shard_map/ppermute | solution.py:24
  124.9 6.1 %collective-permute-done.7 = f32[256,512]{1,0:T(8,128)S(1)} collective-permute-done((f32[256,512]{1,0:T(8,128)S(1)}, f32[256,512]{1,0:T(8,128)S(1)}, u32[]{:S(2)}, u32[]{:S(2)}) %collective-permute-start.7) | collective-permute-done | bytes 524320 | tf_op jit(solution)/shard_map/ppermute | solution.py:24
  133.5 2.1 %collective-permute-start.10 = (f32[256,512]{1,0:T(8,128)S(1)}, f32[256,512]{1,0:T(8,128)S(1)}, u32[]{:S(2)}, u32[]{:S(2)}) collective-permute-start(f32[256,512]{1,0:T(8,128)S(1)} %broadcast_select_fusion.1), channel_id=1, source_target_pairs={{0,4},{4,0},{1,5},{5,1},{2,6},{6,2},{3,7},{7,3},{8,12},{12,8},{9,1... | collective-permute-start | bytes 1572872 | tf_op jit(solution)/shard_map/ppermute | solution.py:24
  135.7 1.9 %collective-permute-done.12 = f32[256,512]{1,0:T(8,128)} collective-permute-done((f32[256,512]{1,0:T(8,128)S(1)}, f32[256,512]{1,0:T(8,128)}, u32[]{:S(2)}, u32[]{:S(2)}) %collective-permute-start.12) | collective-permute-done | bytes 524320 | tf_op jit(solution)/shard_map/ppermute | solution.py:24
  137.7 1.1 broadcast_select_fusion.9
  138.8 1.9 %convolution_bitcast_fusion = f32[256,512]{0,1:T(8,128)S(1)} fusion(f32[256,512]{1,0:T(8,128)S(1)} %get-tuple-element.31, f32[256,512]{1,0:T(8,128)S(1)} %get-tuple-element.32, bf16[3,1,512,256]{3,2,1,0:T(8,128)(2,1)} %param.21), kind=kOutput, calls=%fused_computation.23 | convolution fusion | flops 805568512 | bytes 1835008 | tf_op jit(solution)/shard_map/dot_general | solution.py:112
  141.8 7.5 %collective-permute-done.10 = f32[256,512]{1,0:T(8,128)S(1)} collective-permute-done((f32[256,512]{1,0:T(8,128)S(1)}, f32[256,512]{1,0:T(8,128)S(1)}, u32[]{:S(2)}, u32[]{:S(2)}) %collective-permute-start.10) | collective-permute-done | bytes 524320 | tf_op jit(solution)/shard_map/ppermute | solution.py:24
  (120 shorter events, 29.1 us)
Async XLA Ops:
  0.6 31.1 %copy-start = (bf16[512,256]{1,0:T(8,128)(2,1)S(1)}, bf16[512,256]{1,0:T(8,128)(2,1)}, u32[]{:S(2)}) copy-start(bf16[512,256]{1,0:T(8,128)(2,1)} %param.19) | copy-start | bytes 786436
  0.6 57.8 %collective-permute-start.3 = (bf16[512,512]{1,0:T(8,128)(2,1)}, bf16[512,512]{1,0:T(8,128)(2,1)S(1)}, u32[]{:S(2)}, u32[]{:S(2)}) collective-permute-start(bf16[512,512]{1,0:T(8,128)(2,1)} %param.16), channel_id=1, source_target_pairs={{32,0},{64,32},{96,64},{128,96},{160,128},{192,160},{224,192},{256... | collective-permute-start | bytes 1572872 | tf_op jit(solution)/shard_map/ppermute | solution.py:14
  11.4 47.8 %collective-permute-start.2 = (bf16[512,512]{1,0:T(8,128)(2,1)}, bf16[512,512]{1,0:T(8,128)(2,1)}, u32[]{:S(2)}, u32[]{:S(2)}) collective-permute-start(bf16[512,512]{1,0:T(8,128)(2,1)} %param.16), channel_id=1, source_target_pairs={{480,0},{0,32},{32,64},{64,96},{96,128},{128,160},{160,192},{192,2... | collective-permute-start | bytes 1572872 | tf_op jit(solution)/shard_map/ppermute | solution.py:14
  13.4 22.1 %collective-permute-start.1 = (bf16[3,512]{1,0:T(4,128)(2,1)}, bf16[3,512]{1,0:T(4,128)(2,1)S(1)}, u32[]{:S(2)}, u32[]{:S(2)}) collective-permute-start(bf16[3,512]{1,0:T(4,128)(2,1)} %param.15), channel_id=1, source_target_pairs={{32,0},{64,32},{96,64},{128,96},{160,128},{192,160},{224,192},{256... | collective-permute-start | bytes 9224 | tf_op jit(solution)/shard_map/ppermute | solution.py:14
  20.6 14.9 %collective-permute-start = (bf16[3,512]{1,0:T(4,128)(2,1)}, bf16[3,512]{1,0:T(4,128)(2,1)S(1)}, u32[]{:S(2)}, u32[]{:S(2)}) collective-permute-start(bf16[3,512]{1,0:T(4,128)(2,1)} %param.15), channel_id=1, source_target_pairs={{480,0},{0,32},{32,64},{64,96},{96,128},{128,160},{160,192},{192,2... | collective-permute-start | bytes 9224 | tf_op jit(solution)/shard_map/ppermute | solution.py:14
  25.7 7.6 %collective-permute-start.5 = (f32[3,256]{0,1:T(8,128)S(1)}, f32[3,256]{0,1:T(8,128)S(1)}, u32[]{:S(2)}, u32[]{:S(2)}) collective-permute-start(f32[3,256]{0,1:T(8,128)S(1)} %select_bitcast_fusion.2), channel_id=1, source_target_pairs={{0,1},{1,0},{2,3},{3,2},{4,5},{5,4},{6,7},{7,6},{8,9},{9,8},{10,11... | collective-permute-start | bytes 9224 | tf_op jit(solution)/shard_map/ppermute | solution.py:24
  31.1 22.4 %copy-start.10 = (pred[256]{0:T(512)(128)(4,1)}, pred[256]{0:T(512)(128)(4,1)S(1)}, u32[]{:S(2)}) copy-start(pred[256]{0:T(512)(128)(4,1)S(1)} %compare_and_fusion.2) | copy-start | bytes 772
  33.3 43.8 %collective-permute-start.6 = (f32[256,512]{1,0:T(8,128)S(1)}, f32[256,512]{1,0:T(8,128)}, u32[]{:S(2)}, u32[]{:S(2)}) collective-permute-start(f32[256,512]{1,0:T(8,128)S(1)} %fusion.94), channel_id=1, source_target_pairs={{0,1},{1,0},{2,3},{3,2},{4,5},{5,4},{6,7},{7,6},{8,9},{9,8},{10,11... | collective-permute-start | bytes 1572872 | tf_op jit(solution)/shard_map/ppermute | solution.py:24
  39.3 14.2 %collective-permute-start.8 = (f32[3,256]{0,1:T(8,128)S(1)}, f32[3,256]{0,1:T(8,128)S(1)}, u32[]{:S(2)}, u32[]{:S(2)}) collective-permute-start(f32[3,256]{0,1:T(8,128)S(1)} %select_bitcast_fusion.1), channel_id=1, source_target_pairs={{0,2},{2,0},{1,3},{3,1},{4,6},{6,4},{5,7},{7,5},{8,10},{10,8},{9,1... | collective-permute-start | bytes 9224 | tf_op jit(solution)/shard_map/ppermute | solution.py:24
  49.9 9.4 %copy-start.6 = (bf16[512,512]{1,0:T(8,128)(2,1)S(1)}, bf16[512,512]{1,0:T(8,128)(2,1)}, u32[]{:S(2)}) copy-start(bf16[512,512]{1,0:T(8,128)(2,1)} %param.16) | copy-start | bytes 1572868
  55.3 36.4 %collective-permute-start.11 = (f32[3,256]{0,1:T(8,128)}, f32[3,256]{0,1:T(8,128)}, u32[]{:S(2)}, u32[]{:S(2)}) collective-permute-start(f32[3,256]{0,1:T(8,128)} %select_bitcast_fusion), channel_id=1, source_target_pairs={{0,4},{4,0},{1,5},{5,1},{2,6},{6,2},{3,7},{7,3},{8,12},{12,8},{9,1... | collective-permute-start | bytes 9224 | tf_op jit(solution)/shard_map/ppermute | solution.py:24
  58.5 0.8 copy-start.9
  66.7 1.7 %copy-start.2 = (bf16[2,256,512]{2,1,0:T(8,128)(2,1)S(1)}, bf16[2,256,512]{2,1,0:T(8,128)(2,1)}, u32[]{:S(2)}) copy-start(bf16[2,256,512]{2,1,0:T(8,128)(2,1)} %gather_fusion.5) | copy-start | bytes 1572868
  66.7 1.7 %copy-start.5 = (f32[2,256,256]{2,1,0:T(8,128)S(1)}, f32[2,256,256]{2,1,0:T(8,128)}, u32[]{:S(2)}) copy-start(f32[2,256,256]{2,1,0:T(8,128)} %get-tuple-element.20) | copy-start | bytes 1572868
  68.3 1.0 copy-start.1
  68.3 1.2 copy-start.4
  68.8 1.2 copy-start.3
  69.9 1.0 copy-start.7
  69.9 1.2 copy-start.8
  73.7 10.7 %collective-permute-start.4 = (f32[256,512]{1,0:T(8,128)S(1)}, f32[256,512]{1,0:T(8,128)S(1)}, u32[]{:S(2)}, u32[]{:S(2)}) collective-permute-start(f32[256,512]{1,0:T(8,128)S(1)} %broadcast_select_fusion.3), channel_id=1, source_target_pairs={{0,1},{1,0},{2,3},{3,2},{4,5},{5,4},{6,7},{7,6},{8,9},{9,8},{10,11... | collective-permute-start | bytes 1572872 | tf_op jit(solution)/shard_map/ppermute | solution.py:24
  79.9 40.0 %collective-permute-start.9 = (f32[256,512]{1,0:T(8,128)S(1)}, f32[256,512]{1,0:T(8,128)}, u32[]{:S(2)}, u32[]{:S(2)}) collective-permute-start(f32[256,512]{1,0:T(8,128)S(1)} %convolution_bitcast_fusion.2), channel_id=1, source_target_pairs={{0,2},{2,0},{1,3},{3,1},{4,6},{6,4},{5,7},{7,5},{8,10},{10,8},{9,1... | collective-permute-start | bytes 1572872 | tf_op jit(solution)/shard_map/ppermute | solution.py:24
  85.8 1.0 copy-start.11
  86.9 44.1 %collective-permute-start.7 = (f32[256,512]{1,0:T(8,128)S(1)}, f32[256,512]{1,0:T(8,128)S(1)}, u32[]{:S(2)}, u32[]{:S(2)}) collective-permute-start(f32[256,512]{1,0:T(8,128)S(1)} %broadcast_select_fusion.2), channel_id=1, source_target_pairs={{0,2},{2,0},{1,3},{3,1},{4,6},{6,4},{5,7},{7,5},{8,10},{10,8},{9,1... | collective-permute-start | bytes 1572872 | tf_op jit(solution)/shard_map/ppermute | solution.py:24
  122.6 15.0 %collective-permute-start.12 = (f32[256,512]{1,0:T(8,128)S(1)}, f32[256,512]{1,0:T(8,128)}, u32[]{:S(2)}, u32[]{:S(2)}) collective-permute-start(f32[256,512]{1,0:T(8,128)S(1)} %convolution_bitcast_fusion.1), channel_id=1, source_target_pairs={{0,4},{4,0},{1,5},{5,1},{2,6},{6,2},{3,7},{7,3},{8,12},{12,8},{9,1... | collective-permute-start | bytes 1572872 | tf_op jit(solution)/shard_map/ppermute | solution.py:24
  133.5 15.7 %collective-permute-start.10 = (f32[256,512]{1,0:T(8,128)S(1)}, f32[256,512]{1,0:T(8,128)S(1)}, u32[]{:S(2)}, u32[]{:S(2)}) collective-permute-start(f32[256,512]{1,0:T(8,128)S(1)} %broadcast_select_fusion.1), channel_id=1, source_target_pairs={{0,4},{4,0},{1,5},{5,1},{2,6},{6,2},{3,7},{7,3},{8,12},{12,8},{9,1... | collective-permute-start | bytes 1572872 | tf_op jit(solution)/shard_map/ppermute | solution.py:24
  150.7 1.0 copy-start.12
where the time goes:
time: 154 us; the launch traced here: 153 us
  starting transfers between devices  55.1 us (36%)
  waiting for transfers between devices  45.9 us (30%)
  local copies, waits for them, and re-layouts  21.7 us (14%)
  matrix products  14.9 us (10%)
  other arithmetic  13.6 us (9%)
    ppermute x9, waiting for transfers between devices, swapped(): return lax.ppermute(block, axis, route)  45.9 us
    ppermute x9, starting transfers between devices, swapped(): return lax.ppermute(block, axis, route)  33.2 us
    ppermute x4, starting transfers between devices, shifted(): return lax.ppermute(block, axis, route)  21.9 us
    gather x5, local copies, waits for them, and re-layouts, on_device(): jnp.take(wide_blocks, candidate, axis=0)  6.08 us
    dot_general x3, matrix products, on_device(): lax.dot_general(projection, jnp.concatenate([left_compressed, right_compr...  5.24 us
    dot_general x5, matrix products, on_device(): jnp.einsum('ipq,iqr->ipr', near_block, jnp.take(wide_blocks, candidate, a...  4.28 us
    unnamed x28, local copies, waits for them, and re-layouts  4.25 us
    select_n x3, other arithmetic, on_device(): right_compressed = jnp.where(is_left, other_compressed, compressed)  3.4 us
  transfers between devices with their start and end apart: 13, of which 5 were waited for; matrix products, arithmetic and copies ran while one was open for 29% of the time, Pallas kernels for 0%

commit v1 on v0

v1 whole, which is shorter than its diff:
```python
import functools
import math

import jax
import jax.numpy as jnp
from jax import lax
from jax.experimental import pallas as pl
from jax.experimental.pallas import tpu as pltpu
from jax.sharding import PartitionSpec as P

SPREAD = 25.0
MESH = pl.DeviceIdType.MESH
BF = jnp.bfloat16
F32 = jnp.float32
FAR = -512.0
SCALE = 2.0 * SPREAD / math.log(2.0)
N_CHUNK = 4


def tdot(a, b):
    return lax.dot_general(a, b, (((0,), (0,)), ((), ())), preferred_element_type=F32)


def mdot(a, b):
    return jnp.dot(a, b, preferred_element_type=F32)


def rows_of(shape, entries):
    index = lax.broadcasted_iota(jnp.int32, shape, 0)
    result = jnp.zeros(shape, F32)
    for at, value in entries:
        result = jnp.where(index == at, value, result)
    return result


def features(points, block_rows):
    count = points.shape[1]
    x, y, z = points[0:1], points[1:2], points[2:3]
    half = 0.5 * (x * x + y * y + z * z)
    high = half.astype(BF).astype(F32)
    mid = (half - high).astype(BF).astype(F32)
    low = (half - high - mid).astype(BF).astype(F32)
    lane = lax.broadcasted_iota(jnp.int32, (1, count), 1)
    in_first = (lane < block_rows).astype(F32)
    return rows_of(
        (16, count),
        [(0, x), (1, y), (2, z), (3, 1.0), (4, 1.0), (5, 1.0), (6, high), (7, mid), (8, low),
         (9, in_first), (10, 1.0 - in_first)],
    )


def source_side(feat, penalties):
    r = lax.broadcasted_iota(jnp.int32, (16, 16), 0)
    c = lax.broadcasted_iota(jnp.int32, (16, 16), 1)
    same = (r == c) & (r < 3)
    swap = ((r >= 3) & (r < 6) & (c == r + 3)) | ((r >= 6) & (r < 9) & (c == r - 3))
    form = jnp.where(same, 1.0, jnp.where(swap, -1.0, 0.0)).astype(BF)
    turned = mdot(form, feat)
    return (turned + rows_of(turned.shape, penalties + [(11, FAR)])).astype(BF)


def only_valid(feat):
    index = lax.broadcasted_iota(jnp.int32, feat.shape, 0)
    return jnp.where(index == 11, 1.0 - feat[3:4], feat).astype(BF)


def kernel_of(target, source, amp):
    return jnp.exp2(tdot(target, source) * SCALE + math.log2(amp))


def one_hot(pivots, offset, count):
    k = lax.broadcasted_iota(jnp.int32, (count, pivots.shape[1]), 0)
    return jnp.where(k == pivots - offset, 1.0, 0.0).astype(BF)


def body(n_blk, near_amp, far_amp,
         lists, points, pivots, tree_pivots, test_hbm, proj_hbm, tree_hbm,
         sample, top, omega,
         wide, proj, tree, near, part, feat_own, feat_in, u0, v0, u1, v1, u2, v2,
         c0, c1, c2, e2, e3, f_out, f_core, g_out, g_in, h_out, h_in, own_sum,
         local_sem, send_sem, recv_sem):
    b = lax.axis_index("blk")
    l = lax.axis_index("leaf")
    core = lax.rem(l, 2)
    bits = [lax.rem(l // (1 << t), 2) for t in range(3)]
    peers = {
        "next": {"blk": lax.rem(b + 1, n_blk), "leaf": l},
        "prev": {"blk": lax.rem(b + n_blk - 1, n_blk), "leaf": l},
    }
    for t in range(3):
        peers[t] = {"blk": b, "leaf": l + (1 << t) - (2 << t) * bits[t]}
    barrier = pltpu.get_barrier_semaphore()
    for peer in peers.values():
        pl.semaphore_signal(barrier, inc=1, device_id=peer, device_id_type=MESH)

    rows = proj.shape[0]
    block_rows = rows // 2
    rank = proj.shape[1]
    half_rank = rank // 2
    cols = wide.shape[1] // N_CHUNK
    used = [0]
    pending = []

    def send(src, dst, peer):
        at = used[0]
        used[0] += 1
        copy = pltpu.make_async_remote_copy(
            src_ref=src, dst_ref=dst, send_sem=send_sem.at[at], recv_sem=recv_sem.at[at],
            device_id=peers[peer], device_id_type=MESH)
        copy.start()
        pending.append(copy)
        return copy

    fetch = [
        pltpu.make_async_copy(test_hbm, wide.at[pl.ds(rows, rows), :], local_sem.at[0]),
        pltpu.make_async_copy(proj_hbm, proj, local_sem.at[1]),
        pltpu.make_async_copy(tree_hbm, tree, local_sem.at[2]),
    ]
    for copy in fetch:
        copy.start()

    own = features(points[...].astype(F32), block_rows).astype(BF)
    feat_own[...] = own
    skeleton = mdot(own, one_hot(pivots[...], 0, rows)).astype(BF)
    u0[...] = skeleton
    pick_own = [one_hot(tree_pivots[t], rank * bits[t], rank) for t in range(3)]
    pick_sib = [one_hot(tree_pivots[t], rank * (1 - bits[t]), rank) for t in range(3)]

    pl.semaphore_wait(barrier, len(peers))

    far_feat = [send(feat_own, feat_in.at[0], "next"), send(feat_own, feat_in.at[1], "prev")]
    u0_copy = send(u0, v0, 0)
    stream = []
    for j in range(N_CHUNK):
        at = pl.ds(j * cols, cols)
        stream.append((
            send(test_hbm.at[:, at], wide.at[pl.ds(0, rows), at], "next"),
            send(test_hbm.at[:, at], wide.at[pl.ds(2 * rows, rows), at], "prev"),
        ))

    fetch[0].wait()
    fetch[1].wait()
    c0[...] = tdot(proj[...], wide[rows:2 * rows, :]).astype(BF)
    c0_copy = send(c0, wide.at[pl.ds(3 * rows, rank), :], 0)

    def hit(i, c):
        found = lists[i, 0] == c
        for e in range(1, lists.shape[1]):
            found = found | (lists[i, e] == c)
        return jnp.where(found, 0.0, FAR)

    def near_source(feat, group):
        lane = lax.broadcasted_iota(jnp.int32, (1, rows), 1)
        penalties = [
            (9 + i, jnp.where(lane < block_rows, hit(i, 2 * group), hit(i, 2 * group + 1)))
            for i in range(2)
        ]
        return source_side(feat, penalties)

    near[:, rows:2 * rows] = kernel_of(own, near_source(own, 1), near_amp).astype(BF)
    w1 = mdot(skeleton, pick_own[0])
    w2 = mdot(w1.astype(BF), pick_own[1])
    w3 = mdot(w2.astype(BF), pick_own[2])
    mine = only_valid(w3)

    fetch[2].wait()
    u0_copy.wait_recv()
    sib0 = v0[...]
    level1 = (w1 + mdot(sib0, pick_sib[0])).astype(BF)
    u1[...] = level1
    c0_copy.wait_recv()

    def merged(t, mine_ref, sib_ref):
        left = tree[t, pl.ds(pl.multiple_of(rank * bits[t], rank), rank), :]
        right = tree[t, pl.ds(pl.multiple_of(rank * (1 - bits[t]), rank), rank), :]
        return tdot(left, mine_ref[...]) + tdot(right, sib_ref[...])

    low_half = pl.ds(pl.multiple_of(core * half_rank, half_rank), half_rank)
    own_rows = pl.ds(pl.multiple_of(rank + core * half_rank, half_rank), half_rank)
    c1[rank:, :] = merged(0, c0, wide.at[pl.ds(3 * rows, rank), :]).astype(BF)
    u1_copy = send(u1, v1, 1)
    c1_copy = send(c1.at[own_rows, :], c1.at[low_half, :], 1)

    part[:, 2 * rows:] = -kernel_of(mine, source_side(sib0, []), far_amp).astype(BF)
    for copy in far_feat:
        copy.wait_recv()
    for g in range(2):
        source = near_source(feat_in[g], 2 * g)
        part[:, g * rows:(g + 1) * rows] = kernel_of(mine, source, near_amp).astype(BF)
        near[:, 2 * g * rows:(2 * g + 1) * rows] = kernel_of(own, source, near_amp).astype(BF)

    f_copy, g_copy, h_copy, t_copy = {}, {}, {}, {}
    far_half = pl.ds(pl.multiple_of((1 - core) * half_rank, half_rank), half_rank)

    def leaf_rows(j):
        at = slice(j * cols, (j + 1) * cols)
        for copy in stream[j]:
            copy.wait_recv()
        total = mdot(part[:, :rows], wide[:rows, at]) + mdot(part[:, rows:], wide[2 * rows:, at])
        f_out[j] = total.astype(BF)
        f_copy[j] = send(f_out.at[j, far_half, :], f_core.at[j], 0)

    def block_rows_sum(j):
        at = slice(j * cols, (j + 1) * cols)
        sample[:, at] = mdot(near[...], wide[:3 * rows, at]).astype(BF)

    def chip_rows(j):
        f_copy[j].wait_recv()
        g_out[j] = (f_out[j, low_half, :].astype(F32) + f_core[j].astype(F32)).astype(BF)
        g_copy[j] = send(g_out.at[j], g_in.at[j], 1)

    def node_rows(j):
        at = slice(j * cols, (j + 1) * cols)
        g_copy[j].wait_recv()
        total = g_out[j].astype(F32) + g_in[j].astype(F32) - e2[:, at]
        own_sum[j] = total
        h_out[j] = total.astype(BF)
        h_copy[j] = send(h_out.at[j], h_in.at[j], 2)

    def top_rows(j):
        at = slice(j * cols, (j + 1) * cols)
        h_copy[j].wait_recv()
        top[low_half, at] = own_sum[j] + h_in[j].astype(F32) - e3[:, at]
        place = top.at[low_half, pl.ds(j * cols, cols)]
        t_copy[j] = send(place, place, 0)

    def halves(feat):
        return jnp.where(core == 0, feat[:, :half_rank], feat[:, half_rank:])

    def correction(mine_feat, sib_feat, sib_skel, own_skel, stacked):
        weights = jnp.concatenate(
            [kernel_of(only_valid(halves(mine_feat)), source_side(sib_skel, []), far_amp).astype(BF),
             kernel_of(only_valid(halves(sib_feat)), source_side(own_skel, []), far_amp).astype(BF)],
            axis=1)
        return mdot(weights, stacked[...])

    leaf_rows(0)
    block_rows_sum(0)
    chip_rows(0)
    leaf_rows(1)
    chip_rows(1)
    block_rows_sum(1)

    u1_copy.wait_recv()
    sib1 = v1[...]
    from_own = mdot(level1, pick_own[1])
    from_sib = mdot(sib1, pick_sib[1])
    level2 = (from_own + from_sib).astype(BF)
    u2[...] = level2
    u2_copy = send(u2, v2, 2)
    c1_copy.wait_recv()
    c1_share = send(c1.at[low_half, :], c1.at[low_half, :], 0)
    x2 = mdot(from_own.astype(BF), pick_own[2])
    y2 = mdot(from_sib.astype(BF), pick_own[2])

    leaf_rows(2)
    chip_rows(2)

    c1_share.wait_recv()
    c2[rank:, :] = merged(1, c1.at[pl.ds(rank, rank), :], c1.at[pl.ds(0, rank), :]).astype(BF)
    c2_copy = send(c2.at[own_rows, :], c2.at[low_half, :], 2)
    e2[...] = correction(x2, y2, sib1, level1, c1)
    block_rows_sum(2)
    node_rows(0)
    node_rows(1)

    leaf_rows(3)
    chip_rows(3)
    block_rows_sum(3)

    u2_copy.wait_recv()
    sib2 = v2[...]
    y3 = mdot(sib2, pick_sib[2])
    c2_copy.wait_recv()
    c2_share = send(c2.at[low_half, :], c2.at[low_half, :], 0)
    node_rows(2)
    c2_share.wait_recv()
    e3[...] = correction(x2 + y2, y3, sib2, level2, c2)
    top_rows(0)
    top_rows(1)
    omega[...] = merged(2, c2.at[pl.ds(rank, rank), :], c2.at[pl.ds(0, rank), :])
    node_rows(3)
    top_rows(2)
    top_rows(3)
    for j in range(N_CHUNK):
        t_copy[j].wait_recv()
    for copy in pending:
        copy.wait_send()


def on_device(n_blk, points, test_matrix, near_lists, leaf_pivots, leaf_proj, merge_pivots, merge_proj):
    rows, cols = test_matrix.shape
    rank = leaf_pivots.shape[1]
    slots = near_lists.shape[1]
    near_amp = 9.0 / math.sqrt(slots * (rows // near_lists.shape[0]))
    far_amp = 3.0 / math.sqrt(rank)
    half = rank // 2
    chunk = cols // N_CHUNK
    vmem = pl.BlockSpec(memory_space=pltpu.VMEM)
    anyw = pl.BlockSpec(memory_space=pl.ANY)
    copies = 14 + 6 * N_CHUNK
    scratch = [
        pltpu.VMEM((3 * rows + rank, cols), BF),
        pltpu.VMEM((rows, rank), BF),
        pltpu.VMEM((3, 2 * rank, rank), BF),
        pltpu.VMEM((rows, 3 * rows), BF),
        pltpu.VMEM((rank, 2 * rows + rank), BF),
        pltpu.VMEM((16, rows), BF),
        pltpu.VMEM((2, 16, rows), BF),
    ] + [pltpu.VMEM((16, rank), BF)] * 6 + [
        pltpu.VMEM((rank, cols), BF),
        pltpu.VMEM((2 * rank, cols), BF),
        pltpu.VMEM((2 * rank, cols), BF),
        pltpu.VMEM((half, cols), F32),
        pltpu.VMEM((half, cols), F32),
        pltpu.VMEM((N_CHUNK, rank, chunk), BF),
    ] + [pltpu.VMEM((N_CHUNK, half, chunk), BF)] * 5 + [
        pltpu.VMEM((N_CHUNK, half, chunk), F32),
        pltpu.SemaphoreType.DMA((3,)),
        pltpu.SemaphoreType.DMA((copies,)),
        pltpu.SemaphoreType.DMA((copies,)),
    ]
    return pl.pallas_call(
        functools.partial(body, n_blk, near_amp, far_amp),
        name="hss",
        out_shape=(
            jax.ShapeDtypeStruct((rows, cols), BF),
            jax.ShapeDtypeStruct((rank, cols), F32),
            jax.ShapeDtypeStruct((rank, cols), F32),
        ),
        in_specs=[pl.BlockSpec(memory_space=pltpu.SMEM), vmem, vmem, vmem, anyw, anyw, anyw],
        out_specs=(vmem, vmem, vmem),
        scratch_shapes=scratch,
        compiler_params=pltpu.CompilerParams(
            collective_id=0, has_side_effects=True, vmem_limit_bytes=48 << 20),
    )(near_lists, points, leaf_pivots, merge_pivots, test_matrix, leaf_proj,
      merge_proj.reshape(merge_proj.shape[0], merge_proj.shape[2], merge_proj.shape[3]))


def solution(mesh):
    placed = (
        P(None, ("blk", "leaf")),
        P(("blk", "leaf"), None),
        P(("blk", "leaf"), None),
        P(("blk", "leaf"), None),
        P(("blk", "leaf"), None),
        P(None, ("blk", "leaf"), None),
        P(None, ("blk", "leaf"), None, None),
    )
    return jax.shard_map(
        functools.partial(on_device, mesh.shape["blk"]),
        mesh=mesh,
        in_specs=placed,
        out_specs=(P(("blk", "leaf"), None), P(("blk", "leaf"), None), P(("blk", "leaf"), None)),
        check_vma=False,
    )
```

time: 154 us -> 58 us (0.38)
  the two profiles are of different devices: /device:TPU:1 before, /device:TPU:87 now
where the time goes in v1:
time: 58 us; the launch traced here: 57.6 us
  Pallas kernels  48.8 us (84%)
  local copies, waits for them, and re-layouts  8.22 us (14%)
  between operations  0.66 us (1%)
    pallas_call x1, Pallas kernels, on_device(): pl.pallas_call(functools.partial(body, n_blk, near_amp, far_amp), name='h...  48.8 us
    unnamed x17, local copies, waits for them, and re-layouts  8.22 us

profile of v1, /device:TPU:87, one launch (start us, length us, event | category | flops | bytes accessed | tf_op | source)
XLA Modules:
  0.0 57.6 jit_solution(6268294809626492963)
XLA Ops:
  0.6 0.0 copy-start.5
  0.6 0.7 %copy-done.5 = s32[2,5]{1,0:T(2,128)S(1)} copy-done((s32[2,5]{1,0:T(2,128)S(1)}, s32[2,5]{1,0:T(2,128)}, u32[]{:S(2)}) %copy-start.5) | copy-done | bytes 64
  1.3 0.0 copy-start
  1.3 1.1 %copy-done = bf16[3,1,512,256]{3,2,1,0:T(8,128)(2,1)S(1)} copy-done((bf16[3,1,512,256]{3,2,1,0:T(8,128)(2,1)S(1)}, bf16[3,1,512,256]{3,2,1,0:T(8,128)(2,1)}, u32[]{:S(2)}) %copy-start) | copy-done | bytes 786456
  2.4 0.0 copy-start.1
  2.4 1.0 %copy-done.1 = bf16[512,512]{1,0:T(8,128)(2,1)S(1)} copy-done((bf16[512,512]{1,0:T(8,128)(2,1)S(1)}, bf16[512,512]{1,0:T(8,128)(2,1)}, u32[]{:S(2)}) %copy-start.1) | copy-done | bytes 524312
  3.5 0.0 copy-start.2
  3.5 0.9 %copy-done.2 = bf16[512,256]{1,0:T(8,128)(2,1)S(1)} copy-done((bf16[512,256]{1,0:T(8,128)(2,1)S(1)}, bf16[512,256]{1,0:T(8,128)(2,1)}, u32[]{:S(2)}) %copy-start.2) | copy-done | bytes 262168
  4.4 0.0 copy-start.3
  4.4 0.7 %copy-done.3 = bf16[3,512]{1,0:T(4,128)(2,1)S(1)} copy-done((bf16[3,512]{1,0:T(4,128)(2,1)S(1)}, bf16[3,512]{1,0:T(4,128)(2,1)}, u32[]{:S(2)}) %copy-start.3) | copy-done | bytes 3096
  5.1 0.0 copy-start.4
  5.1 0.7 %copy-done.4 = s32[3,1,256]{2,1,0:T(1,128)S(1)} copy-done((s32[3,1,256]{2,1,0:T(1,128)S(1)}, s32[3,1,256]{2,1,0:T(1,128)}, u32[]{:S(2)}) %copy-start.4) | copy-done | bytes 3096
  5.8 0.0 copy-start.6
  5.8 0.7 %copy-done.6 = s32[1,256]{1,0:T(1,128)S(1)} copy-done((s32[1,256]{1,0:T(1,128)S(1)}, s32[1,256]{1,0:T(1,128)}, u32[]{:S(2)}) %copy-start.6) | copy-done | bytes 1048
  6.5 48.8 %hss.1 = (bf16[512,512]{1,0:T(8,128)(2,1)S(1)}, f32[256,512]{1,0:T(8,128)S(1)}, f32[256,512]{1,0:T(8,128)S(1)}) custom-call(s32[2,5]{1,0:T(2,128)S(1)} %copy-done.5, bf16[3,512]{1,0:T(4,128)(2,1)S(1)} %copy-done.3, s32[1,256]{1,0:T(1,128)S(1)} %copy-done.6, s32[3,1,256]{2,1,0:T(1,128)S(1)} %copy-done.4, bf16[512,512]{1,0:T(8,128)(2,1)S(1)} %copy-done.1, ...), custom_call_target="tpu_custom_call" | custom-call | tf_op jit(solution)/shard_map/hss/pallas_call | solution.py:323
  55.3 0.8 %copy.13 = bf16[512,512]{1,0:T(8,128)(2,1)} copy(bf16[512,512]{1,0:T(8,128)(2,1)S(1)} %get-tuple-element.6) | data formatting | bytes 1048576
  56.0 0.8 %copy.14 = f32[256,512]{1,0:T(8,128)} copy(f32[256,512]{1,0:T(8,128)S(1)} %get-tuple-element.7) | data formatting | bytes 1048576
  56.8 0.8 %copy.15 = f32[256,512]{1,0:T(8,128)} copy(f32[256,512]{1,0:T(8,128)S(1)} %get-tuple-element.8) | data formatting | bytes 1048576
Async XLA Ops:
  0.6 0.7 %copy-start.5 = (s32[2,5]{1,0:T(2,128)S(1)}, s32[2,5]{1,0:T(2,128)}, u32[]{:S(2)}) copy-start(s32[2,5]{1,0:T(2,128)} %lists.1) | copy-start | bytes 124
  1.3 1.1 %copy-start = (bf16[3,1,512,256]{3,2,1,0:T(8,128)(2,1)S(1)}, bf16[3,1,512,256]{3,2,1,0:T(8,128)(2,1)}, u32[]{:S(2)}) copy-start(bf16[3,1,512,256]{3,2,1,0:T(8,128)(2,1)} %param.13) | copy-start | bytes 2359300
  2.4 1.0 %copy-start.1 = (bf16[512,512]{1,0:T(8,128)(2,1)S(1)}, bf16[512,512]{1,0:T(8,128)(2,1)}, u32[]{:S(2)}) copy-start(bf16[512,512]{1,0:T(8,128)(2,1)} %test_hbm.1) | copy-start | bytes 1572868
  3.5 0.9 %copy-start.2 = (bf16[512,256]{1,0:T(8,128)(2,1)S(1)}, bf16[512,256]{1,0:T(8,128)(2,1)}, u32[]{:S(2)}) copy-start(bf16[512,256]{1,0:T(8,128)(2,1)} %proj_hbm.1) | copy-start | bytes 786436
  4.4 0.7 %copy-start.3 = (bf16[3,512]{1,0:T(4,128)(2,1)S(1)}, bf16[3,512]{1,0:T(4,128)(2,1)}, u32[]{:S(2)}) copy-start(bf16[3,512]{1,0:T(4,128)(2,1)} %points.1) | copy-start | bytes 9220
  5.1 0.7 %copy-start.4 = (s32[3,1,256]{2,1,0:T(1,128)S(1)}, s32[3,1,256]{2,1,0:T(1,128)}, u32[]{:S(2)}) copy-start(s32[3,1,256]{2,1,0:T(1,128)} %tree_pivots.1) | copy-start | bytes 9220
  5.8 0.7 %copy-start.6 = (s32[1,256]{1,0:T(1,128)S(1)}, s32[1,256]{1,0:T(1,128)}, u32[]{:S(2)}) copy-start(s32[1,256]{1,0:T(1,128)} %pivots.1) | copy-start | bytes 3076

commit v2 on v0

v2 whole, which is shorter than its diff:
```python
import functools
import math

import jax
import jax.numpy as jnp
from jax import lax
from jax.experimental import pallas as pl
from jax.experimental.pallas import tpu as pltpu
from jax.sharding import PartitionSpec as P

SPREAD = 25.0
MESH = pl.DeviceIdType.MESH
BF = jnp.bfloat16
F32 = jnp.float32
FAR = -512.0
SCALE = 2.0 * SPREAD / math.log(2.0)


def tdot(a, b):
    return lax.dot_general(a, b, (((0,), (0,)), ((), ())), preferred_element_type=F32)


def mdot(a, b):
    return jnp.dot(a, b, preferred_element_type=F32)


def rows_of(shape, entries):
    index = lax.broadcasted_iota(jnp.int32, shape, 0)
    result = jnp.zeros(shape, F32)
    for at, value in entries:
        result = jnp.where(index == at, value, result)
    return result


PLACES = ((9, 10), (14, 15), (12, 13))


def features(points, lists, block_rows):
    count = points.shape[1]
    x, y, z = points[0:1], points[1:2], points[2:3]
    half = 0.5 * (x * x + y * y + z * z)
    high = half.astype(BF).astype(F32)
    mid = (half - high).astype(BF).astype(F32)
    low = (half - high - mid).astype(BF).astype(F32)
    lane = lax.broadcasted_iota(jnp.int32, (1, count), 1)
    entries = [(0, x), (1, y), (2, z), (3, 1.0), (4, 1.0), (5, 1.0), (6, high), (7, mid), (8, low)]
    for place, at in enumerate(PLACES):
        for j in range(2):
            listed = jnp.max((lists == 2 * place + j).astype(F32), axis=1, keepdims=True)
            skipped = (1.0 - listed) * FAR
            entries.append((at[j], jnp.where(lane < block_rows, skipped[0:1], skipped[1:2])))
    return rows_of((16, count), entries)


def source_side(feat, place=None):
    r = lax.broadcasted_iota(jnp.int32, (16, 16), 0)
    c = lax.broadcasted_iota(jnp.int32, (16, 16), 1)
    same = (r == c) & (r < 3)
    swap = ((r >= 3) & (r < 6) & (c == r + 3)) | ((r >= 6) & (r < 9) & (c == r - 3))
    form = jnp.where(same, 1.0, jnp.where(swap, -1.0, 0.0)).astype(BF)
    turned = mdot(form, feat)
    count = feat.shape[1]
    extra = [(11, FAR)]
    if place is not None:
        lane = lax.broadcasted_iota(jnp.int32, (1, count), 1)
        first = (lane < count // 2).astype(F32)
        extra += [(PLACES[place][0], first), (PLACES[place][1], 1.0 - first)]
    return (turned + rows_of(turned.shape, extra)).astype(BF)


def only_valid(feat):
    index = lax.broadcasted_iota(jnp.int32, feat.shape, 0)
    return jnp.where(index == 11, 1.0 - feat[3:4], feat).astype(BF)


def kernel_of(target, source, amp):
    return jnp.exp2(tdot(target, source) * SCALE + math.log2(amp))


def one_hot(pivots, offset, count):
    k = lax.broadcasted_iota(jnp.int32, (count, pivots.shape[1]), 0)
    return jnp.where(k == pivots - offset, 1.0, 0.0).astype(BF)


def body(n_blk, near_amp, far_amp,
         lists_hbm, points_hbm, pivots_hbm, tree_pivots_hbm, test_hbm, proj_hbm, tree_hbm,
         sample, top, omega,
         lists, points, pivots, tree_pivots, proj, tree, wide, stack, near, far,
         feat_out, feat_in, kept_out, kept_in, chip_out, z_in, y_in, yz_in,
         o_out, o_core, o_sum, o_q, o_part, o_y, o_send, o_z, o_t, o_ty, o_tc,
         r_out, r_core, r_sum, r_x, e_out, e_core,
         g_half, g_own, g_part, g_y, g_out, g_z, g_t, g_ty, g_tc,
         local_sem, send_sem, recv_sem):
    b = lax.axis_index("blk")
    l = lax.axis_index("leaf")
    bits = [lax.rem(l // (1 << t), 2) for t in range(3)]
    step = [(1 << t) - (2 << t) * bits[t] for t in range(3)]
    peers = {
        "next": {"blk": lax.rem(b + 1, n_blk), "leaf": l},
        "prev": {"blk": lax.rem(b + n_blk - 1, n_blk), "leaf": l},
        "core": {"blk": b, "leaf": l + step[0]},
        "z": {"blk": b, "leaf": l + step[1]},
        "y": {"blk": b, "leaf": l + step[2]},
        "yz": {"blk": b, "leaf": l + step[1] + step[2]},
    }
    barrier = pltpu.get_barrier_semaphore()
    for peer in peers.values():
        pl.semaphore_signal(barrier, inc=1, device_id=peer, device_id_type=MESH)

    rows, rank = proj.shape
    block_rows = rows // 2
    half = rank // 2
    quarter = half // 2
    pending = []

    def send(src, dst, peer):
        at = len(pending)
        copy = pltpu.make_async_remote_copy(
            src_ref=src, dst_ref=dst, send_sem=send_sem.at[at], recv_sem=recv_sem.at[at],
            device_id=peers[peer], device_id_type=MESH)
        copy.start()
        pending.append(copy)
        return copy

    def fetch(at, src, dst):
        copy = pltpu.make_async_copy(src, dst, local_sem.at[at])
        copy.start()
        return copy

    small = [fetch(0, lists_hbm, lists), fetch(1, points_hbm, points),
             fetch(2, pivots_hbm, pivots), fetch(3, tree_pivots_hbm, tree_pivots)]
    large = [fetch(4, test_hbm, wide.at[pl.ds(rows, rows), :]), fetch(5, proj_hbm, proj),
             fetch(6, tree_hbm, tree)]

    near_half = pl.ds(pl.multiple_of(bits[0] * half, half), half)
    far_half = pl.ds(pl.multiple_of((1 - bits[0]) * half, half), half)
    near_quarter = pl.ds(pl.multiple_of(bits[2] * quarter, quarter), quarter)
    far_quarter = pl.ds(pl.multiple_of((1 - bits[2]) * quarter, quarter), quarter)

    def quarter_of(core, part):
        return pl.ds(pl.multiple_of(core * half + part * quarter, quarter), quarter)

    top_quarter = quarter_of(bits[0], bits[2])

    for copy in small:
        copy.wait()
    own = features(points[...].astype(F32), lists[...], block_rows).astype(BF)
    skeleton = mdot(own, one_hot(pivots[...], 0, rows)).astype(BF)
    kept = skeleton
    for t in range(3):
        kept = mdot(kept, one_hot(tree_pivots[t], rank * bits[t], rank)).astype(BF)
        kept_out[:, t * rank:(t + 1) * rank] = kept
    feat_out[:, :rows] = own
    feat_out[:, rows:] = only_valid(kept.astype(F32))

    pl.semaphore_wait(barrier, len(peers))

    kept_copy = send(kept_out, kept_in, "core")
    feat_copy = [send(feat_out, feat_in.at[0], "next"), send(feat_out, feat_in.at[1], "prev")]

    def stream_chunk(start, size):
        at = pl.ds(start, size)
        return [
            send(test_hbm.at[:, at], wide.at[pl.ds(0, rows), at], "next"),
            send(test_hbm.at[:, at], wide.at[pl.ds(2 * rows, rows), at], "prev"),
        ]

    cols = wide.shape[1]
    stream = [stream_chunk(0, cols // 4)]

    for copy in large:
        copy.wait()
    share = tdot(proj[...], wide[rows:2 * rows, :])

    kept_copy.wait_recv()
    chip = kept_out[...].astype(F32) + kept_in[...].astype(F32)
    level1 = chip[:, :rank].astype(BF)
    chip_out[...] = chip[:, rank:].astype(BF)
    chip_copy = [
        send(chip_out, z_in, "z"),
        send(chip_out.at[:, pl.ds(rank, rank)], yz_in, "yz"),
        send(chip_out.at[:, pl.ds(rank, rank)], y_in, "y"),
    ]

    for t in range(3):
        high = share.astype(BF)
        low = (share - high.astype(F32)).astype(BF)
        stack[t * rank:(t + 1) * rank, :] = high
        child = tree[t, 0, pl.ds(pl.multiple_of(rank * bits[t], rank), rank), :]
        share = tdot(child, high) + tdot(child, low)
    o_out[...] = share
    o_core_copy = send(o_out.at[far_half, :], o_core, "core")

    for copy in feat_copy:
        copy.wait_recv()
    for side, place in ((0, 2), (1, 0)):
        weights = kernel_of(feat_in[side, :, rows:], source_side(own, place), near_amp).astype(BF)
        r_out[side] = mdot(weights, wide[rows:2 * rows, :]).astype(BF)
    r_core_copy = send(r_out.at[:, far_half, :], r_core, "core")

    o_core_copy.wait_recv()
    o_sum[...] = o_out[near_half, :] + o_core[...]
    o_part[...] = o_sum[far_quarter, :].astype(BF)
    o_y_copy = send(o_part, o_y, "y")

    r_core_copy.wait_recv()
    r_sum[...] = (r_out[:, near_half, :].astype(F32) + r_core[...].astype(F32)).astype(BF)
    r_x_copy = [send(r_sum.at[1], r_x.at[0], "next"), send(r_sum.at[0], r_x.at[1], "prev")]
    stream.append(stream_chunk(cols // 4, cols // 4))
    stream.append(stream_chunk(cols // 2, cols // 2))

    def weigh(t, feat, source):
        at = slice(t * rank, (t + 1) * rank)
        far[:, at] = kernel_of(only_valid(feat), source_side(source), far_amp).astype(BF)

    def near_part(place, feat):
        at = slice(place * rows, (place + 1) * rows)
        near[:, at] = kernel_of(own, source_side(feat, place), near_amp).astype(BF)

    weigh(0, kept_in[:, 2 * rank:].astype(F32), skeleton)
    near_part(1, own)

    o_y_copy.wait_recv()
    o_q[...] = o_sum[near_quarter, :] + o_y[...].astype(F32)
    o_send[...] = o_q[...].astype(BF)
    o_z_copy = send(o_send, o_z, "z")

    chip_copy[0].wait_recv()
    weigh(1, z_in[:, rank:].astype(F32), level1)
    level2 = (chip_out[:, :rank].astype(F32) + z_in[:, :rank].astype(F32)).astype(BF)
    chip_copy[1].wait_recv()
    chip_copy[2].wait_recv()
    weigh(2, y_in[...].astype(F32) + yz_in[...].astype(F32), level2)
    e_out[...] = mdot(far[...], stack[...]).astype(BF)
    e_core_copy = send(e_out.at[far_half, :], e_core, "core")

    near_part(0, feat_in[0, :, :rows])

    e_core_copy.wait_recv()
    for copy in r_x_copy:
        copy.wait_recv()
    g_half[...] = (r_x[0].astype(F32) + r_x[1].astype(F32)
                   - (e_out[near_half, :].astype(F32) + e_core[...].astype(F32)))
    g_part[...] = g_half[far_quarter, :].astype(BF)
    g_y_copy = send(g_part, g_y, "y")

    near_part(2, feat_in[1, :, :rows])

    g_y_copy.wait_recv()
    g_own[...] = g_half[near_quarter, :] + g_y[...].astype(F32)
    g_out[...] = g_own[...].astype(BF)
    g_z_copy = send(g_out, g_z, "z")

    def spread(total, result, t_out, t_y):
        result[top_quarter, :] = total
        t_out[...] = total.astype(BF)
        place = result.at[top_quarter, :]
        return send(t_out, t_y, "y"), send(place, place, "core")

    def collect(copies, result, t_y, t_core):
        copies[0].wait_recv()
        last = send(t_y, t_core, "core")
        result[quarter_of(bits[0], 1 - bits[2]), :] = t_y[...].astype(F32)
        return last

    def finish(copies, last, result, t_core):
        copies[1].wait_recv()
        last.wait_recv()
        result[quarter_of(1 - bits[0], 1 - bits[2]), :] = t_core[...].astype(F32)

    def block_rows_sum(chunks, start, size):
        at = slice(start, start + size)
        for j in chunks:
            for copy in stream[j]:
                copy.wait_recv()
        sample[:, at] = mdot(near[...], wide[:, at]).astype(BF)

    o_z_copy.wait_recv()
    o_spread = spread(o_q[...] + o_z[...].astype(F32), omega, o_t, o_ty)
    block_rows_sum((0, 1), 0, cols // 2)
    o_last = collect(o_spread, omega, o_ty, o_tc)

    g_z_copy.wait_recv()
    g_spread = spread(g_own[...] + g_z[...].astype(F32), top, g_t, g_ty)
    finish(o_spread, o_last, omega, o_tc)
    g_last = collect(g_spread, top, g_ty, g_tc)

    block_rows_sum((2,), cols // 2, cols // 2)
    finish(g_spread, g_last, top, g_tc)
    for copy in pending:
        copy.wait_send()


def write_out(a, b, c, a_out, b_out, c_out, sem):
    copies = [pltpu.make_async_copy(src, dst, sem.at[i])
              for i, (src, dst) in enumerate(((a, a_out), (b, b_out), (c, c_out)))]
    for copy in copies:
        copy.start()
    for copy in copies:
        copy.wait()


def on_device(n_blk, points, test_matrix, near_lists, leaf_pivots, leaf_proj, merge_pivots, merge_proj):
    rows, cols = test_matrix.shape
    rank = leaf_pivots.shape[1]
    slots = near_lists.shape[1]
    near_amp = 9.0 / math.sqrt(slots * (rows // near_lists.shape[0]))
    far_amp = 3.0 / math.sqrt(rank)
    half = rank // 2
    quarter = rank // 4
    vmem = pl.BlockSpec(memory_space=pltpu.VMEM)
    hbm = pl.BlockSpec(memory_space=pltpu.HBM)
    anyw = pl.BlockSpec(memory_space=pl.ANY)
    copies = 28
    scratch = [
        pltpu.VMEM(near_lists.shape, jnp.int32),
        pltpu.VMEM(points.shape, BF),
        pltpu.VMEM(leaf_pivots.shape, jnp.int32),
        pltpu.VMEM(merge_pivots.shape, jnp.int32),
        pltpu.VMEM(leaf_proj.shape, BF),
        pltpu.VMEM(merge_proj.shape, BF),
        pltpu.VMEM((3 * rows, cols), BF),
        pltpu.VMEM((3 * rank, cols), BF),
        pltpu.VMEM((rows, 3 * rows), BF),
        pltpu.VMEM((rank, 3 * rank), BF),
        pltpu.VMEM((16, rows + rank), BF),
        pltpu.VMEM((2, 16, rows + rank), BF),
        pltpu.VMEM((16, 3 * rank), BF),
        pltpu.VMEM((16, 3 * rank), BF),
        pltpu.VMEM((16, 2 * rank), BF),
        pltpu.VMEM((16, 2 * rank), BF),
        pltpu.VMEM((16, rank), BF),
        pltpu.VMEM((16, rank), BF),
        pltpu.VMEM((rank, cols), F32),
        pltpu.VMEM((half, cols), F32),
        pltpu.VMEM((half, cols), F32),
        pltpu.VMEM((quarter, cols), F32),
    ] + [pltpu.VMEM((quarter, cols), BF)] * 7 + [
        pltpu.VMEM((2, rank, cols), BF),
        pltpu.VMEM((2, half, cols), BF),
        pltpu.VMEM((2, half, cols), BF),
        pltpu.VMEM((2, half, cols), BF),
        pltpu.VMEM((rank, cols), BF),
        pltpu.VMEM((half, cols), BF),
        pltpu.VMEM((half, cols), F32),
        pltpu.VMEM((quarter, cols), F32),
    ] + [pltpu.VMEM((quarter, cols), BF)] * 7 + [
        pltpu.SemaphoreType.DMA((7,)),
        pltpu.SemaphoreType.DMA((copies,)),
        pltpu.SemaphoreType.DMA((copies,)),
    ]
    shapes = (
        jax.ShapeDtypeStruct((rows, cols), BF),
        jax.ShapeDtypeStruct((rank, cols), F32),
        jax.ShapeDtypeStruct((rank, cols), F32),
    )
    operands = [
        pltpu.with_memory_space_constraint(v, pltpu.HBM)
        for v in (near_lists, points, leaf_pivots, merge_pivots, test_matrix, leaf_proj, merge_proj)
    ]
    made = pl.pallas_call(
        functools.partial(body, n_blk, near_amp, far_amp),
        name="hss",
        out_shape=shapes,
        in_specs=[hbm] * 7,
        out_specs=(vmem, vmem, vmem),
        scratch_shapes=scratch,
        compiler_params=pltpu.CompilerParams(
            collective_id=0, has_side_effects=True, vmem_limit_bytes=40 << 20),
    )(*operands)
    return pl.pallas_call(
        write_out,
        name="write_out",
        out_shape=shapes,
        in_specs=[anyw] * 3,
        out_specs=(anyw, anyw, anyw),
        scratch_shapes=[pltpu.SemaphoreType.DMA((3,))],
        compiler_params=pltpu.CompilerParams(vmem_limit_bytes=1 << 20),
    )(*made)


def solution(mesh):
    placed = (
        P(None, ("blk", "leaf")),
        P(("blk", "leaf"), None),
        P(("blk", "leaf"), None),
        P(("blk", "leaf"), None),
        P(("blk", "leaf"), None),
        P(None, ("blk", "leaf"), None),
        P(None, ("blk", "leaf"), None, None),
    )
    return jax.shard_map(
        functools.partial(on_device, mesh.shape["blk"]),
        mesh=mesh,
        in_specs=placed,
        out_specs=(P(("blk", "leaf"), None), P(("blk", "leaf"), None), P(("blk", "leaf"), None)),
        check_vma=False,
    )
```

time: 154 us -> 47 us (0.31)
  starting transfers between devices: 55.1 us -> 0 us
  Pallas kernels: 0 us -> 46.2 us
  waiting for transfers between devices: 45.9 us -> 0 us
  local copies, waits for them, and re-layouts: 21.7 us -> 0 us
  matrix products: 14.9 us -> 0 us
  other arithmetic: 13.6 us -> 0 us
    ppermute x13 -> x0, starting transfers between devices: 55.1 us -> none  [the longest x9 33.2 us: swapped(): return lax.ppermute(block, axis, route)]
    pallas_call x0 -> x2, Pallas kernels: none -> 46.2 us  [the longest x1 45.1 us: on_device(): pl.pallas_call(functools.partial(body, n_blk, near_amp, far_amp), name='h...]
    ppermute x13 -> x0, waiting for transfers between devices: 45.9 us -> none  [the longest x9 45.9 us: swapped(): return lax.ppermute(block, axis, route)]
    gather x17 -> x0, local copies, waits for them, and re-layouts: 15 us -> none  [the longest x5 6.08 us: on_device(): jnp.take(wide_blocks, candidate, axis=0)]
    dot_general x15 -> x0, matrix products: 14.9 us -> none  [the longest x3 5.24 us: on_device(): lax.dot_general(projection, jnp.concatenate([left_compressed, right_compr...]
    select_n x25 -> x0, other arithmetic: 7.85 us -> none  [the longest x3 3.4 us: on_device(): right_compressed = jnp.where(is_left, other_compressed, compressed)]
    unnamed x28 -> x0, local copies, waits for them, and re-layouts: 4.25 us -> none
    reduce_sum x4 -> x0, other arithmetic: 2.81 us -> none  [kernel_block(): return jnp.exp(-SPREAD * jnp.sum(offsets * offsets, axis=-3))]
  transfers between devices with their start and end apart: 13 -> 0, of which waited for: 5 -> 0; matrix products, arithmetic and copies ran while one was open for 29% -> 0% of each run, Pallas kernels for 0% -> 0%
where the time goes in v2:
time: 47 us; the launch traced here: 46.9 us
  Pallas kernels  46.2 us (98%)
  between operations  0.64 us (1%)
    pallas_call x1, Pallas kernels, on_device(): pl.pallas_call(functools.partial(body, n_blk, near_amp, far_amp), name='h...  45.1 us
    pallas_call x1, Pallas kernels, on_device(): pl.pallas_call(write_out, name='write_out', out_shape=shapes, in_specs=[a...  1.17 us

profile of v2, /device:TPU:1, one launch (start us, length us, event | category | flops | bytes accessed | tf_op | source)
XLA Modules:
  0.0 46.9 jit_solution(6664346710623353830)
XLA Ops:
  0.6 45.1 %hss.1 = (bf16[512,512]{1,0:T(8,128)(2,1)S(1)}, f32[256,512]{1,0:T(8,128)S(1)}, f32[256,512]{1,0:T(8,128)S(1)}) custom-call(s32[2,5]{1,0:T(2,128)} %lists_hbm.1, bf16[3,512]{1,0:T(4,128)(2,1)} %points_hbm.1, s32[1,256]{1,0:T(1,128)} %pivots_hbm.1, s32[3,1,256]{2,1,0:T(1,128)} %tree_pivots_hbm.1, bf16[512,512]{1,0:T(8,128)(2,1)} %test_hbm.1, ...), custom_call_target="tpu_custom_call" | custom-call | tf_op jit(solution)/shard_map/hss/pallas_call | solution.py:361
  45.7 1.2 %write_out.1 = (bf16[512,512]{1,0:T(8,128)(2,1)}, f32[256,512]{1,0:T(8,128)}, f32[256,512]{1,0:T(8,128)}) custom-call(bf16[512,512]{1,0:T(8,128)(2,1)S(1)} %get-tuple-element.6.a, f32[256,512]{1,0:T(8,128)S(1)} %get-tuple-element.7.b, f32[256,512]{1,0:T(8,128)S(1)} %get-tuple-element.8.c), custom_call_target="tpu_custom_call" | custom-call | tf_op jit(solution)/shard_map/write_out/pallas_call | solution.py:371

commit v3 on v2

--- a/solution.py
+++ b/solution.py
@@ -88,9 +88,9 @@
          lists, points, pivots, tree_pivots, proj, tree, wide, stack, near, far,
          feat_out, feat_in, kept_out, kept_in, chip_out, z_in, y_in, yz_in,
          o_out, o_core, o_sum, o_q, o_part, o_y, o_send, o_z, o_t, o_ty, o_tc,
-         r_out, r_core, r_sum, r_x, e_out, e_core,
-         g_half, g_own, g_part, g_y, g_out, g_z, g_t, g_ty, g_tc,
-         local_sem, send_sem, recv_sem):
+         r_out, r_core, r_sum, r_x, e_out, e_core, g_half, g_own,
+         g_part, g_y, g_out, g_z, t_out, t_y, t_core,
+         hello, local_sem, send_sem, recv_sem):
     b = lax.axis_index("blk")
     l = lax.axis_index("leaf")
     bits = [lax.rem(l // (1 << t), 2) for t in range(3)]
@@ -104,8 +104,14 @@
         "yz": {"blk": b, "leaf": l + step[1] + step[2]},
     }
     barrier = pltpu.get_barrier_semaphore()
-    for peer in peers.values():
-        pl.semaphore_signal(barrier, inc=1, device_id=peer, device_id_type=MESH)
+    upper = bits[1]
+    for name in ("next", "prev", "core", "y"):
+        pl.semaphore_signal(barrier, inc=1, device_id=peers[name], device_id_type=MESH)
+
+    @pl.when(upper == 0)
+    def _():
+        for name in ("z", "yz"):
+            pl.semaphore_signal(barrier, inc=1, device_id=peers[name], device_id_type=MESH)
 
     rows, rank = proj.shape
     block_rows = rows // 2
@@ -113,13 +119,17 @@
     quarter = half // 2
     pending = []
 
-    def send(src, dst, peer):
+    def plan(src, dst, peer):
         at = len(pending)
         copy = pltpu.make_async_remote_copy(
             src_ref=src, dst_ref=dst, send_sem=send_sem.at[at], recv_sem=recv_sem.at[at],
             device_id=peers[peer], device_id_type=MESH)
+        pending.append(copy)
+        return copy
+
+    def send(src, dst, peer):
+        copy = plan(src, dst, peer)
         copy.start()
-        pending.append(copy)
         return copy
 
     def fetch(at, src, dst):
@@ -153,10 +163,23 @@
     feat_out[:, :rows] = own
     feat_out[:, rows:] = only_valid(kept.astype(F32))
 
-    pl.semaphore_wait(barrier, len(peers))
-
+    @pl.when(upper == 0)
+    def _():
+        pl.semaphore_wait(barrier, 4)
+
+    @pl.when(upper == 1)
+    def _():
+        pl.semaphore_wait(barrier, 6)
+        for at, name in enumerate(("z", "yz")):
+            pl.semaphore_signal(hello.at[at], inc=1, device_id=peers[name], device_id_type=MESH)
+
+    feat_copy = [send(feat_out, feat_in.at[0], "next"), send(feat_out, feat_in.at[1], "prev")]
     kept_copy = send(kept_out, kept_in, "core")
-    feat_copy = [send(feat_out, feat_in.at[0], "next"), send(feat_out, feat_in.at[1], "prev")]
+
+    cols = wide.shape[1]
+    wing = cols // 2
+    wings = [pl.ds(h * wing, wing) for h in range(2)]
+    cut = [slice(h * wing, (h + 1) * wing) for h in range(2)]
 
     def stream_chunk(start, size):
         at = pl.ds(start, size)
@@ -165,23 +188,35 @@
             send(test_hbm.at[:, at], wide.at[pl.ds(2 * rows, rows), at], "prev"),
         ]
 
-    cols = wide.shape[1]
-    stream = [stream_chunk(0, cols // 4)]
-
-    for copy in large:
-        copy.wait()
-    share = tdot(proj[...], wide[rows:2 * rows, :])
+    stream = [stream_chunk(0, wing)]
 
     kept_copy.wait_recv()
     chip = kept_out[...].astype(F32) + kept_in[...].astype(F32)
     level1 = chip[:, :rank].astype(BF)
     chip_out[...] = chip[:, rank:].astype(BF)
+    last_rank = pl.ds(rank, rank)
     chip_copy = [
-        send(chip_out, z_in, "z"),
-        send(chip_out.at[:, pl.ds(rank, rank)], yz_in, "yz"),
-        send(chip_out.at[:, pl.ds(rank, rank)], y_in, "y"),
+        plan(chip_out, z_in, "z"),
+        plan(chip_out.at[:, last_rank], yz_in, "yz"),
+        send(chip_out.at[:, last_rank], y_in, "y"),
     ]
 
+    @pl.when(upper == 1)
+    def _():
+        for copy in chip_copy[:2]:
+            copy.start()
+
+    for copy in large:
+        copy.wait()
+
+    r_core_copy = []
+    for side, place in ((0, 2), (1, 0)):
+        feat_copy[side].wait_recv()
+        weights = kernel_of(feat_in[side, :, rows:], source_side(own, place), near_amp).astype(BF)
+        r_out[side] = mdot(weights, wide[rows:2 * rows, :]).astype(BF)
+        r_core_copy.append(send(r_out.at[side, far_half, :], r_core.at[side], "core"))
+
+    share = tdot(proj[...], wide[rows:2 * rows, :])
     for t in range(3):
         high = share.astype(BF)
         low = (share - high.astype(F32)).astype(BF)
@@ -189,104 +224,125 @@
         child = tree[t, 0, pl.ds(pl.multiple_of(rank * bits[t], rank), rank), :]
         share = tdot(child, high) + tdot(child, low)
     o_out[...] = share
+
+    r_x_copy = [[], []]
+    for side, name in ((0, "prev"), (1, "next")):
+        r_core_copy[side].wait_recv()
+        r_sum[side] = (r_out[side, near_half, :].astype(F32) + r_core[side].astype(F32)).astype(BF)
+        for h, at in enumerate(wings):
+            r_x_copy[h].append(send(r_sum.at[side, :, at], r_x.at[1 - side, :, at], name))
     o_core_copy = send(o_out.at[far_half, :], o_core, "core")
 
-    for copy in feat_copy:
-        copy.wait_recv()
-    for side, place in ((0, 2), (1, 0)):
-        weights = kernel_of(feat_in[side, :, rows:], source_side(own, place), near_amp).astype(BF)
-        r_out[side] = mdot(weights, wide[rows:2 * rows, :]).astype(BF)
-    r_core_copy = send(r_out.at[:, far_half, :], r_core, "core")
+    def weigh(t, feat, source):
+        at = slice(t * rank, (t + 1) * rank)
+        far[:, at] = kernel_of(only_valid(feat), source_side(source), far_amp).astype(BF)
+
+    def near_part(place, feat):
+        at = slice(place * rows, (place + 1) * rows)
+        near[:, at] = kernel_of(own, source_side(feat, place), near_amp).astype(BF)
+
+    weigh(0, kept_in[:, 2 * rank:].astype(F32), skeleton)
+    near_part(1, own)
 
     o_core_copy.wait_recv()
     o_sum[...] = o_out[near_half, :] + o_core[...]
     o_part[...] = o_sum[far_quarter, :].astype(BF)
     o_y_copy = send(o_part, o_y, "y")
 
-    r_core_copy.wait_recv()
-    r_sum[...] = (r_out[:, near_half, :].astype(F32) + r_core[...].astype(F32)).astype(BF)
-    r_x_copy = [send(r_sum.at[1], r_x.at[0], "next"), send(r_sum.at[0], r_x.at[1], "prev")]
-    stream.append(stream_chunk(cols // 4, cols // 4))
-    stream.append(stream_chunk(cols // 2, cols // 2))
-
-    def weigh(t, feat, source):
-        at = slice(t * rank, (t + 1) * rank)
-        far[:, at] = kernel_of(only_valid(feat), source_side(source), far_amp).astype(BF)
-
-    def near_part(place, feat):
-        at = slice(place * rows, (place + 1) * rows)
-        near[:, at] = kernel_of(own, source_side(feat, place), near_amp).astype(BF)
-
-    weigh(0, kept_in[:, 2 * rank:].astype(F32), skeleton)
-    near_part(1, own)
-
+    @pl.when(upper == 0)
+    def _():
+        for at in range(2):
+            pl.semaphore_wait(hello.at[at], 1)
+        for copy in chip_copy[:2]:
+            copy.start()
+
+    near_part(0, feat_in[0, :, :rows])
+
+    for copy in chip_copy:
+        copy.wait_recv()
+    weigh(1, z_in[:, rank:].astype(F32), level1)
+    level2 = (chip_out[:, :rank].astype(F32) + z_in[:, :rank].astype(F32)).astype(BF)
+    weigh(2, y_in[...].astype(F32) + yz_in[...].astype(F32), level2)
+    e_out[...] = mdot(far[...], stack[...]).astype(BF)
+    e_core_copy = send(e_out.at[far_half, :], e_core, "core")
     o_y_copy.wait_recv()
     o_q[...] = o_sum[near_quarter, :] + o_y[...].astype(F32)
     o_send[...] = o_q[...].astype(BF)
     o_z_copy = send(o_send, o_z, "z")
 
-    chip_copy[0].wait_recv()
-    weigh(1, z_in[:, rank:].astype(F32), level1)
-    level2 = (chip_out[:, :rank].astype(F32) + z_in[:, :rank].astype(F32)).astype(BF)
-    chip_copy[1].wait_recv()
-    chip_copy[2].wait_recv()
-    weigh(2, y_in[...].astype(F32) + yz_in[...].astype(F32), level2)
-    e_out[...] = mdot(far[...], stack[...]).astype(BF)
-    e_core_copy = send(e_out.at[far_half, :], e_core, "core")
-
-    near_part(0, feat_in[0, :, :rows])
+    g_y_copy, g_z_copy, t_y_copy, t_core_copy, t_last = {}, {}, {}, {}, {}
+
+    def y_stage(h):
+        at = cut[h]
+        for copy in r_x_copy[h]:
+            copy.wait_recv()
+        g_half[:, at] = r_x[0, :, at].astype(F32) + r_x[1, :, at].astype(F32) - g_half[:, at]
+        g_part[:, at] = g_half[far_quarter, at].astype(BF)
+        g_y_copy[h] = send(g_part.at[:, wings[h]], g_y.at[:, wings[h]], "y")
+
+    def z_stage(h):
+        at = cut[h]
+        g_y_copy[h].wait_recv()
+        g_own[:, at] = g_half[near_quarter, at] + g_y[:, at].astype(F32)
+        g_out[:, at] = g_own[:, at].astype(BF)
+        g_z_copy[h] = send(g_out.at[:, wings[h]], g_z.at[:, wings[h]], "z")
+
+    def top_stage(h):
+        at = cut[h]
+        g_z_copy[h].wait_recv()
+        total = g_own[:, at] + g_z[:, at].astype(F32)
+        top[top_quarter, at] = total
+        t_out[:, at] = total.astype(BF)
+        t_y_copy[h] = send(t_out.at[:, wings[h]], t_y.at[:, wings[h]], "y")
+        place = top.at[top_quarter, wings[h]]
+        t_core_copy[h] = send(place, place, "core")
+
+    def last_stage(h):
+        at = cut[h]
+        t_y_copy[h].wait_recv()
+        t_last[h] = send(t_y.at[:, wings[h]], t_core.at[:, wings[h]], "core")
+        top[quarter_of(bits[0], 1 - bits[2]), at] = t_y[:, at].astype(F32)
+
+    def block_rows_sum(h):
+        for copy in stream[h]:
+            copy.wait_recv()
+        sample[:, cut[h]] = mdot(near[...], wide[:, cut[h]]).astype(BF)
 
     e_core_copy.wait_recv()
-    for copy in r_x_copy:
-        copy.wait_recv()
-    g_half[...] = (r_x[0].astype(F32) + r_x[1].astype(F32)
-                   - (e_out[near_half, :].astype(F32) + e_core[...].astype(F32)))
-    g_part[...] = g_half[far_quarter, :].astype(BF)
-    g_y_copy = send(g_part, g_y, "y")
+    g_half[...] = e_out[near_half, :].astype(F32) + e_core[...].astype(F32)
+    y_stage(0)
+    y_stage(1)
+    z_stage(0)
+    z_stage(1)
+    stream.append(stream_chunk(wing, wing))
 
     near_part(2, feat_in[1, :, :rows])
-
-    g_y_copy.wait_recv()
-    g_own[...] = g_half[near_quarter, :] + g_y[...].astype(F32)
-    g_out[...] = g_own[...].astype(BF)
-    g_z_copy = send(g_out, g_z, "z")
-
-    def spread(total, result, t_out, t_y):
-        result[top_quarter, :] = total
-        t_out[...] = total.astype(BF)
-        place = result.at[top_quarter, :]
-        return send(t_out, t_y, "y"), send(place, place, "core")
-
-    def collect(copies, result, t_y, t_core):
-        copies[0].wait_recv()
-        last = send(t_y, t_core, "core")
-        result[quarter_of(bits[0], 1 - bits[2]), :] = t_y[...].astype(F32)
-        return last
-
-    def finish(copies, last, result, t_core):
-        copies[1].wait_recv()
-        last.wait_recv()
-        result[quarter_of(1 - bits[0], 1 - bits[2]), :] = t_core[...].astype(F32)
-
-    def block_rows_sum(chunks, start, size):
-        at = slice(start, start + size)
-        for j in chunks:
-            for copy in stream[j]:
-                copy.wait_recv()
-        sample[:, at] = mdot(near[...], wide[:, at]).astype(BF)
-
+    block_rows_sum(0)
+
+    top_stage(0)
+    top_stage(1)
     o_z_copy.wait_recv()
-    o_spread = spread(o_q[...] + o_z[...].astype(F32), omega, o_t, o_ty)
-    block_rows_sum((0, 1), 0, cols // 2)
-    o_last = collect(o_spread, omega, o_ty, o_tc)
-
-    g_z_copy.wait_recv()
-    g_spread = spread(g_own[...] + g_z[...].astype(F32), top, g_t, g_ty)
-    finish(o_spread, o_last, omega, o_tc)
-    g_last = collect(g_spread, top, g_ty, g_tc)
-
-    block_rows_sum((2,), cols // 2, cols // 2)
-    finish(g_spread, g_last, top, g_tc)
+    total = o_q[...] + o_z[...].astype(F32)
+    omega[top_quarter, :] = total
+    o_t[...] = total.astype(BF)
+    o_t_copy = send(o_t, o_ty, "y")
+    place = omega.at[top_quarter, :]
+    o_own_copy = send(place, place, "core")
+    last_stage(0)
+    last_stage(1)
+    o_t_copy.wait_recv()
+    o_last = send(o_ty, o_tc, "core")
+    omega[quarter_of(bits[0], 1 - bits[2]), :] = o_ty[...].astype(F32)
+    block_rows_sum(1)
+
+    other = quarter_of(1 - bits[0], 1 - bits[2])
+    for h in range(2):
+        t_core_copy[h].wait_recv()
+        t_last[h].wait_recv()
+    top[other, :] = t_core[...].astype(F32)
+    o_own_copy.wait_recv()
+    o_last.wait_recv()
+    omega[other, :] = o_tc[...].astype(F32)
     for copy in pending:
         copy.wait_send()
 
@@ -311,7 +367,7 @@
     vmem = pl.BlockSpec(memory_space=pltpu.VMEM)
     hbm = pl.BlockSpec(memory_space=pltpu.HBM)
     anyw = pl.BlockSpec(memory_space=pl.ANY)
-    copies = 28
+    copies = 40
     scratch = [
         pltpu.VMEM(near_lists.shape, jnp.int32),
         pltpu.VMEM(points.shape, BF),
@@ -345,6 +401,7 @@
         pltpu.VMEM((half, cols), F32),
         pltpu.VMEM((quarter, cols), F32),
     ] + [pltpu.VMEM((quarter, cols), BF)] * 7 + [
+        pltpu.SemaphoreType.REGULAR((2,)),
         pltpu.SemaphoreType.DMA((7,)),
         pltpu.SemaphoreType.DMA((copies,)),
         pltpu.SemaphoreType.DMA((copies,)),

time: 47 us -> 45.6 us (0.970)
  the two profiles are of different devices: /device:TPU:1 before, /device:TPU:145 now
where the time goes in v3:
time: 45.6 us; the launch traced here: 45.5 us
  Pallas kernels  44.8 us (98%)
  between operations  0.64 us (1%)
    pallas_call x1, Pallas kernels, on_device(): pl.pallas_call(functools.partial(body, n_blk, near_amp, far_amp), name='h...  43.7 us
    pallas_call x1, Pallas kernels, on_device(): pl.pallas_call(write_out, name='write_out', out_shape=shapes, in_specs=[a...  1.17 us

profile of v3, /device:TPU:145, one launch (start us, length us, event | category | flops | bytes accessed | tf_op | source)
XLA Modules:
  0.0 45.5 jit_solution(8795311698417083247)
XLA Ops:
  0.6 43.7 %hss.1 = (bf16[512,512]{1,0:T(8,128)(2,1)S(1)}, f32[256,512]{1,0:T(8,128)S(1)}, f32[256,512]{1,0:T(8,128)S(1)}) custom-call(s32[2,5]{1,0:T(2,128)} %lists_hbm.1, bf16[3,512]{1,0:T(4,128)(2,1)} %points_hbm.1, s32[1,256]{1,0:T(1,128)} %pivots_hbm.1, s32[3,1,256]{2,1,0:T(1,128)} %tree_pivots_hbm.1, bf16[512,512]{1,0:T(8,128)(2,1)} %test_hbm.1, ...), custom_call_target="tpu_custom_call" | custom-call | tf_op jit(solution)/shard_map/hss/pallas_call | solution.py:418
  44.3 1.2 %write_out.1 = (bf16[512,512]{1,0:T(8,128)(2,1)}, f32[256,512]{1,0:T(8,128)}, f32[256,512]{1,0:T(8,128)}) custom-call(bf16[512,512]{1,0:T(8,128)(2,1)S(1)} %get-tuple-element.6.a, f32[256,512]{1,0:T(8,128)S(1)} %get-tuple-element.7.b, f32[256,512]{1,0:T(8,128)S(1)} %get-tuple-element.8.c), custom_call_target="tpu_custom_call" | custom-call | tf_op jit(solution)/shard_map/write_out/pallas_call | solution.py:428

commit v4 on v3

--- a/solution.py
+++ b/solution.py
@@ -188,7 +188,7 @@
             send(test_hbm.at[:, at], wide.at[pl.ds(2 * rows, rows), at], "prev"),
         ]
 
-    stream = [stream_chunk(0, wing)]
+    stream = [stream_chunk(0, wing // 2)]
 
     kept_copy.wait_recv()
     chip = kept_out[...].astype(F32) + kept_in[...].astype(F32)
@@ -303,21 +303,15 @@
         t_last[h] = send(t_y.at[:, wings[h]], t_core.at[:, wings[h]], "core")
         top[quarter_of(bits[0], 1 - bits[2]), at] = t_y[:, at].astype(F32)
 
-    def block_rows_sum(h):
-        for copy in stream[h]:
-            copy.wait_recv()
-        sample[:, cut[h]] = mdot(near[...], wide[:, cut[h]]).astype(BF)
-
     e_core_copy.wait_recv()
     g_half[...] = e_out[near_half, :].astype(F32) + e_core[...].astype(F32)
     y_stage(0)
     y_stage(1)
     z_stage(0)
     z_stage(1)
-    stream.append(stream_chunk(wing, wing))
+    stream.append(stream_chunk(wing // 2, wing + wing // 2))
 
     near_part(2, feat_in[1, :, :rows])
-    block_rows_sum(0)
 
     top_stage(0)
     top_stage(1)
@@ -333,7 +327,11 @@
     o_t_copy.wait_recv()
     o_last = send(o_ty, o_tc, "core")
     omega[quarter_of(bits[0], 1 - bits[2]), :] = o_ty[...].astype(F32)
-    block_rows_sum(1)
+    for part in stream:
+        for copy in part:
+            copy.wait_recv()
+    for at in cut:
+        sample[:, at] = mdot(near[...], wide[:, at]).astype(BF)
 
     other = quarter_of(1 - bits[0], 1 - bits[2])
     for h in range(2):

time: 45.6 us -> 44.2 us (0.969)
  the two profiles are of different devices: /device:TPU:145 before, /device:TPU:1 now
where the time goes in v4:
time: 44.2 us; the launch traced here: 44.1 us
  Pallas kernels  43.4 us (98%)
  between operations  0.64 us (1%)
    pallas_call x1, Pallas kernels, on_device(): pl.pallas_call(functools.partial(body, n_blk, near_amp, far_amp), name='h...  42.3 us
    pallas_call x1, Pallas kernels, on_device(): pl.pallas_call(write_out, name='write_out', out_shape=shapes, in_specs=[a...  1.17 us

profile of v4, /device:TPU:1, one launch (start us, length us, event | category | flops | bytes accessed | tf_op | source)
XLA Modules:
  0.0 44.1 jit_solution(9953065757092907612)
XLA Ops:
  0.6 42.3 %hss.1 = (bf16[512,512]{1,0:T(8,128)(2,1)S(1)}, f32[256,512]{1,0:T(8,128)S(1)}, f32[256,512]{1,0:T(8,128)S(1)}) custom-call(s32[2,5]{1,0:T(2,128)} %lists_hbm.1, bf16[3,512]{1,0:T(4,128)(2,1)} %points_hbm.1, s32[1,256]{1,0:T(1,128)} %pivots_hbm.1, s32[3,1,256]{2,1,0:T(1,128)} %tree_pivots_hbm.1, bf16[512,512]{1,0:T(8,128)(2,1)} %test_hbm.1, ...), custom_call_target="tpu_custom_call" | custom-call | tf_op jit(solution)/shard_map/hss/pallas_call | solution.py:416
  42.9 1.2 %write_out.1 = (bf16[512,512]{1,0:T(8,128)(2,1)}, f32[256,512]{1,0:T(8,128)}, f32[256,512]{1,0:T(8,128)}) custom-call(bf16[512,512]{1,0:T(8,128)(2,1)S(1)} %get-tuple-element.6.a, f32[256,512]{1,0:T(8,128)S(1)} %get-tuple-element.7.b, f32[256,512]{1,0:T(8,128)S(1)} %get-tuple-element.8.c), custom_call_target="tpu_custom_call" | custom-call | tf_op jit(solution)/shard_map/write_out/pallas_call | solution.py:426

commit v5 on v4

--- a/solution.py
+++ b/solution.py
@@ -313,8 +313,6 @@
 
     near_part(2, feat_in[1, :, :rows])
 
-    top_stage(0)
-    top_stage(1)
     o_z_copy.wait_recv()
     total = o_q[...] + o_z[...].astype(F32)
     omega[top_quarter, :] = total
@@ -322,6 +320,8 @@
     o_t_copy = send(o_t, o_ty, "y")
     place = omega.at[top_quarter, :]
     o_own_copy = send(place, place, "core")
+    top_stage(0)
+    top_stage(1)
     last_stage(0)
     last_stage(1)
     o_t_copy.wait_recv()

time: 44.2 us -> 43.5 us (0.984)
  Pallas kernels: 43.4 us -> 42.8 us
    pallas_call x1, Pallas kernels: 42.3 us -> 41.6 us  [on_device(): pl.pallas_call(functools.partial(body, n_blk, near_amp, far_amp), name='h...]
where the time goes in v5:
time: 43.5 us; the launch traced here: 43.4 us
  Pallas kernels  42.8 us (98%)
  between operations  0.64 us (1%)
    pallas_call x1, Pallas kernels, on_device(): pl.pallas_call(functools.partial(body, n_blk, near_amp, far_amp), name='h...  41.6 us
    pallas_call x1, Pallas kernels, on_device(): pl.pallas_call(write_out, name='write_out', out_shape=shapes, in_specs=[a...  1.17 us

profile of v5, /device:TPU:1, one launch (start us, length us, event | category | flops | bytes accessed | tf_op | source)
XLA Modules:
  0.0 43.4 jit_solution(1114432171982997982)
XLA Ops:
  0.6 41.6 %hss.1 = (bf16[512,512]{1,0:T(8,128)(2,1)S(1)}, f32[256,512]{1,0:T(8,128)S(1)}, f32[256,512]{1,0:T(8,128)S(1)}) custom-call(s32[2,5]{1,0:T(2,128)} %lists_hbm.1, bf16[3,512]{1,0:T(4,128)(2,1)} %points_hbm.1, s32[1,256]{1,0:T(1,128)} %pivots_hbm.1, s32[3,1,256]{2,1,0:T(1,128)} %tree_pivots_hbm.1, bf16[512,512]{1,0:T(8,128)(2,1)} %test_hbm.1, ...), custom_call_target="tpu_custom_call" | custom-call | tf_op jit(solution)/shard_map/hss/pallas_call | solution.py:416
  42.2 1.2 %write_out.1 = (bf16[512,512]{1,0:T(8,128)(2,1)}, f32[256,512]{1,0:T(8,128)}, f32[256,512]{1,0:T(8,128)}) custom-call(bf16[512,512]{1,0:T(8,128)(2,1)S(1)} %get-tuple-element.6.a, f32[256,512]{1,0:T(8,128)S(1)} %get-tuple-element.7.b, f32[256,512]{1,0:T(8,128)S(1)} %get-tuple-element.8.c), custom_call_target="tpu_custom_call" | custom-call | tf_op jit(solution)/shard_map/write_out/pallas_call | solution.py:426
